TPU v7x, 32 devices: a whole 2x2x4 slice. The times are simulated.
32 devices in a mesh: ens: 8 (over y, x, core), lon: 4 (over z).
Axes of the slice: x: 2, y: 2, z: 4, core: 2. Of those that a mesh axis runs over, the one named last changes fastest.
Arguments:
- features: bfloat16 [8, 384, 46080], P('ens', None, 'lon'), may hold values from -6 to 6
- proj_weight: bfloat16 [648, 384], replicated, may hold values from -0.3125 to 0.3125
- basis_vals: float32 [32, 32, 9], replicated, may hold values from -0.375 to 0.375
- row_of: int32 [32, 32], replicated, may hold values from 0 to 31
- col_off: int32 [32, 32], replicated, may hold values from -4 to 4
- observed: float32 [72, 46080], P(None, 'lon'), may hold values from -6 to 6
- lat_weight: float32 [32], replicated, may hold values from 0.3 to 1
Outputs:
- feature_grad: bfloat16 [8, 384, 46080], P('ens', None, 'lon')
- weight_grad: float32 [648, 384], replicated
Inputs may be any that keep to these rules, and one draw needn't show every extreme that they name: row_of names a row of the slab. col_off is a longitude offset in columns.
All inputs are finite; a program needn't handle non-finite values.
Results may differ from a plain program's by a relative error of at most 0.0089.
Values may be sent and summed in bfloat16 or wider, within the bound.
A program may use at most 256 MiB of HBM per device.

v0:
```python
import math

import jax
import jax.numpy as jnp
from jax import lax
from jax.sharding import PartitionSpec as P

O = 72
K = 9
R = 4
LAT = 32


SMOOTH = 0.25


def extended(cells, sides, width):
    for axis, dim in sides:
        count = lax.axis_size(axis)
        head = lax.slice_in_dim(cells, 0, width, axis=dim)
        tail = lax.slice_in_dim(cells, cells.shape[dim] - width, cells.shape[dim], axis=dim)
        cells = jnp.concatenate(
            [
                lax.ppermute(tail, axis, [(i, (i + 1) % count) for i in range(count)]),
                cells,
                lax.ppermute(head, axis, [((i + 1) % count, i) for i in range(count)]),
            ],
            axis=dim,
        )
    return cells


def passed_along(value, axis, steps):
    count = lax.axis_size(axis)
    pairs = [(source, (source + steps) % count) for source in range(count)]
    return lax.ppermute(value, axis, pairs)


def kernel_table(basis_vals, row_of, col_off):
    offsets = jnp.arange(2 * R + 1, dtype=jnp.int32) - R
    row_ids = jnp.arange(LAT, dtype=jnp.int32)
    row_hit = (row_of[:, :, None] == row_ids[None, None, :]).astype(jnp.float32)
    col_hit = (col_off[:, :, None] == offsets[None, None, :]).astype(jnp.float32)
    kernel = jnp.einsum(
        "isk,isr,isd->dkir", basis_vals, row_hit, col_hit, precision=lax.Precision.HIGHEST
    )
    return kernel.astype(jnp.bfloat16)


def smooth_slope(diff):
    return diff / jnp.sqrt(diff * diff + SMOOTH * SMOOTH)


def pair_spread(values, others):

    def add_member(index, total):
        single = lax.dynamic_index_in_dim(others, index, 0, keepdims=True)
        return total + smooth_slope(values - single)

    return lax.fori_loop(0, others.shape[0], add_member, jnp.zeros(values.shape, jnp.float32))


def shards(features, proj_weight, basis_vals, row_of, col_off, observed, lat_weight):
    mem_dev = features.shape[0]
    chan_in = features.shape[1]
    cell_count = features.shape[2]
    lon_dev = cell_count // LAT
    rim_cells = R * LAT
    span = lon_dev * O
    kernel = kernel_table(basis_vals, row_of, col_off)
    weight_three = proj_weight.reshape(K, O, chan_in)
    widened = extended(features, (("lon", 2),), rim_cells)
    widened = widened.reshape(mem_dev, chan_in, lon_dev + 2 * R, LAT)
    projected = jnp.einsum(
        "koc,mcjr->mkrjo", weight_three, widened, preferred_element_type=jnp.float32
    ).astype(jnp.bfloat16)
    projected = projected.reshape(mem_dev, K, LAT, (lon_dev + 2 * R) * O)
    decoded = jnp.zeros((mem_dev, LAT, span), jnp.float32)
    for offset in range(2 * R + 1):
        window = projected[:, :, :, offset * O : offset * O + span]
        decoded = decoded + jnp.einsum(
            "kir,mkrx->mix", kernel[offset], window, preferred_element_type=jnp.float32
        )
    flat_out = decoded.reshape(mem_dev, LAT * span)
    observed_flat = observed.reshape(O, lon_dev, LAT).transpose(2, 1, 0).reshape(LAT * span)
    everyone = lax.all_gather(flat_out, "ens", axis=0, tiled=True)
    total_count = everyone.shape[0]
    spread = pair_spread(flat_out, everyone)
    slopes = smooth_slope(flat_out - observed_flat[None, :]) - spread / (total_count - 1)
    cotangent = (slopes.reshape(mem_dev, LAT, span) * lat_weight[None, :, None]).astype(
        jnp.bfloat16
    )
    padded = jnp.pad(cotangent, ((0, 0), (0, 0), (2 * R * O, 2 * R * O)))
    ext_len = (lon_dev + 2 * R) * O
    stacked = jnp.stack(
        [
            padded[:, :, (2 * R - offset) * O : (2 * R - offset) * O + ext_len]
            for offset in range(2 * R + 1)
        ]
    )
    spread_wide = jnp.einsum("dkir,dmix->mkrx", kernel, stacked, preferred_element_type=jnp.float32)
    left_part = spread_wide[:, :, :, : R * O]
    right_part = spread_wide[:, :, :, (lon_dev + R) * O :]
    from_left = passed_along(right_part.astype(jnp.bfloat16), "lon", 1).astype(right_part.dtype)
    from_right = passed_along(left_part.astype(jnp.bfloat16), "lon", -1).astype(left_part.dtype)
    interior = spread_wide[:, :, :, R * O : (lon_dev + R) * O]
    interior = interior.at[:, :, :, : R * O].add(from_left)
    interior = interior.at[:, :, :, span - R * O :].add(from_right)
    grad_local = interior.astype(jnp.bfloat16).reshape(mem_dev, K, LAT, lon_dev, O)
    feature_grad = jnp.einsum(
        "koc,mkrjo->mcjr", weight_three, grad_local, preferred_element_type=jnp.float32
    ).astype(jnp.bfloat16)
    feature_grad = feature_grad.reshape(mem_dev, chan_in, cell_count)
    feature_cells = features.reshape(mem_dev, chan_in, lon_dev, LAT)
    weight_part = jnp.einsum(
        "mkrjo,mcjr->koc", grad_local, feature_cells, preferred_element_type=jnp.float32
    ).reshape(K * O, chan_in)
    members_all = mem_dev * lax.axis_size("ens")
    columns_all = lon_dev * lax.axis_size("lon")
    weight_grad = lax.psum(weight_part, ("ens", "lon")) / math.sqrt(members_all * columns_all * LAT)
    return (feature_grad, weight_grad)


def solution(mesh):
    in_specs = (P("ens", None, "lon"), P(), P(), P(), P(), P(None, "lon"), P())
    out_specs = (P("ens", None, "lon"), P())
    return jax.shard_map(shards, mesh=mesh, in_specs=in_specs, out_specs=out_specs, check_vma=False)
```

profile of v0, /device:TPU:1, one launch (start us, length us, event | category | flops | bytes accessed | tf_op | source)
XLA Modules:
  0.0 896.3 jit_solution(3145240483996057671)
XLA Ops:
  25.8 12.0 %copy.94 = bf16[1,384,11776]{1,2,0:T(8,128)(2,1)} copy(bf16[1,384,11776]{2,1,0:T(8,128)(2,1)} %pad_maximum_fusion) | data formatting | bytes 18087936 | tf_op jit(solution)/shard_map/concatenate | solution.py:22
  37.8 24.2 %convert_bitcast_fusion = bf16[1,9,32,368,72]{4,2,1,3,0:T(8,128)(2,1)} fusion(bf16[384,368,32,1]{0,2,3,1:T(8,128)(2,1)} %bitcast.191, bf16[9,72,384,1]{2,1,0,3:T(8,128)(2,1)S(1)} %bitcast.183), kind=kOutput, calls=%fused_computation.21 | convolution fusion | flops 5868122112 | bytes 24803328 | tf_op jit(solution)/shard_map/koc,mcjr->mkrjo/dot_general | solution.py:74
  62.0 23.9 %copy.95 = bf16[1,9,32,368,72]{4,3,2,1,0:T(8,128)(2,1)} copy(bf16[1,9,32,368,72]{4,2,1,3,0:T(8,128)(2,1)} %convert_bitcast_fusion) | data formatting | bytes 30523392 | tf_op jit(solution)/shard_map/convert_element_type | solution.py:76
  86.0 39.8 %reshape.238 = bf16[1,9,32,26496]{3,2,1,0:T(8,128)(2,1)} reshape(bf16[1,9,32,368,72]{4,3,2,1,0:T(8,128)(2,1)} %copy.95) | data formatting | bytes 30523392 | tf_op jit(solution)/shard_map/reshape | solution.py:77
  173.0 9.3 %fusion.3 = f32[25920,32]{0,1:T(8,128)S(1)} fusion(f32[25920,32]{0,1:T(8,128)S(1)} %convolution_bitcast_fusion.6, f32[25920,32]{0,1:T(8,128)S(1)} %convolution_bitcast_fusion.7, f32[25920,32]{0,1:T(8,128)} %convolution_bitcast_fusion.8, bf16[1,9,32,26496]{3,2,1,0:T(8,128)(2,1)} %reshape.238, bf16[9,32,32]{2,0,1:T(8,128)(2,1)} %get-tuple-element.147), kind=kOutput, calls=%fused_computation.14 | convolution fusion | flops 480245760 | bytes 28377088 | tf_op jit(solution)/shard_map/kir,mkrx->mix/dot_general | solution.py:81
  182.3 12.7 %fusion.6 = f32[25920,32]{0,1:T(8,128)S(1)} fusion(f32[25920,32]{0,1:T(8,128)} %convolution_bitcast_fusion.3, f32[25920,32]{0,1:T(8,128)} %convolution_bitcast_fusion.4, f32[25920,32]{0,1:T(8,128)S(1)} %fusion.3, bf16[1,9,32,26496]{3,2,1,0:T(8,128)(2,1)} %reshape.238, bf16[9,32,32]{2,0,1:T(8,128)(2,1)S(1)} %get-tuple-element.143), kind=kOutput, calls=%fused_computation.17 | convolution fusion | flops 480245760 | bytes 28272640 | tf_op jit(solution)/shard_map/kir,mkrx->mix/dot_general | solution.py:81
  195.1 12.1 %fusion.9 = f32[1,32,25920]{2,1,0:T(8,128)} fusion(f32[25920,32]{0,1:T(8,128)S(1)} %copy-done.6, f32[25920,32]{0,1:T(8,128)S(1)} %fusion.6, bf16[1,9,32,26496]{3,2,1,0:T(8,128)(2,1)} %reshape.238, bf16[9,32,32]{2,0,1:T(8,128)(2,1)S(1)} %copy-done.4), kind=kOutput, calls=%fused_computation.20 | convolution fusion | flops 479416320 | bytes 24938496 | tf_op jit(solution)/shard_map/kir,mkrx->mix/dot_general | solution.py:81
  220.4 9.8 %copy.107 = f32[32,360,72]{2,1,0:T(8,128)} copy(f32[32,360,72]{2,0,1:T(8,128)} %bitcast.190) | data formatting | bytes 6635520 | tf_op jit(solution)/shard_map/transpose | solution.py:85
  230.3 12.0 %broadcast_in_dim_reshape.3 = f32[1,829440]{1,0:T(1,128)} reshape(f32[32,360,72]{2,1,0:T(8,128)} %copy.107) | data formatting | bytes 6635520 | tf_op jit(solution)/shard_map/broadcast_in_dim;reshape | solution.py:89
  250.2 96.0 %all-gather.3.cloned.1.call-done = f32[8,1,829440]{2,1,0:T(1,128)} async-done(((f32[1,1,829440]{2,1,0:T(1,128)}), f32[8,1,829440]{2,1,0:T(1,128)}) %all-gather.3.cloned.1.call-update) | async-done | bytes 26542096 | tf_op jit(solution)/shard_map/all_gather | solution.py:86
  346.1 22.3 %copy.152 = f32[8,1,829440]{2,0,1:T(8,128)} copy(f32[8,1,829440]{2,1,0:T(1,128)} %all-gather.3.cloned.1.call-done) | data formatting | bytes 53084160
  368.4 126.8 %while.16 = (s32[]{:T(128)}, f32[1,829440]{1,0:T(1,128)}, f32[8,829440]{1,0:T(8,128)}, f32[1,829440]{1,0:T(1,128)}, s32[]{:T(128)}, /*index=5*/s32[]{:T(128)}) while((s32[]{:T(128)}, f32[1,829440]{1,0:T(1,128)}, f32[8,829440]{1,0:T(8,128)}, f32[1,829440]{1,0:T(1,128)}, s32[]{:T(128)}, /*index=5*/s32[]{:T(128)}) %tuple.65), condition=%wide.region_1.2_spmd.clone, body=%wide.region_0.1_spmd.clone.sunk | while | flops 4976643 | bytes 13271123 | solution.py:60
  368.4 15.1 %fusion.45 = f32[1,829440]{1,0:T(1,128)} fusion(f32[1,829440]{1,0:T(1,128)} %get-tuple-element.182, pred[]{:T(512)S(6)} %compare.15, f32[1,829440]{1,0:T(1,128)} %get-tuple-element.190, f32[8,829440]{1,0:T(8,128)} %get-tuple-element.189, s32[]{:T(128)} %get-tuple-element.181), kind=kLoop, calls=%fused_computation.1.clone.1 | loop fusion | flops 4976640 | bytes 13271045 | tf_op jit(solution)/shard_map/while/body/eval_jaxpr/add | solution.py:58
  383.5 16.0 %fusion.45 = f32[1,829440]{1,0:T(1,128)} fusion(f32[1,829440]{1,0:T(1,128)} %get-tuple-element.182, pred[]{:T(512)S(6)} %compare.15, f32[1,829440]{1,0:T(1,128)} %get-tuple-element.190, f32[8,829440]{1,0:T(8,128)} %get-tuple-element.189, s32[]{:T(128)} %get-tuple-element.181), kind=kLoop, calls=%fused_computation.1.clone.1 | loop fusion | flops 4976640 | bytes 13271045 | tf_op jit(solution)/shard_map/while/body/eval_jaxpr/add | solution.py:58
  399.5 16.0 %fusion.45 = f32[1,829440]{1,0:T(1,128)} fusion(f32[1,829440]{1,0:T(1,128)} %get-tuple-element.182, pred[]{:T(512)S(6)} %compare.15, f32[1,829440]{1,0:T(1,128)} %get-tuple-element.190, f32[8,829440]{1,0:T(8,128)} %get-tuple-element.189, s32[]{:T(128)} %get-tuple-element.181), kind=kLoop, calls=%fused_computation.1.clone.1 | loop fusion | flops 4976640 | bytes 13271045 | tf_op jit(solution)/shard_map/while/body/eval_jaxpr/add | solution.py:58
  415.4 16.0 %fusion.45 = f32[1,829440]{1,0:T(1,128)} fusion(f32[1,829440]{1,0:T(1,128)} %get-tuple-element.182, pred[]{:T(512)S(6)} %compare.15, f32[1,829440]{1,0:T(1,128)} %get-tuple-element.190, f32[8,829440]{1,0:T(8,128)} %get-tuple-element.189, s32[]{:T(128)} %get-tuple-element.181), kind=kLoop, calls=%fused_computation.1.clone.1 | loop fusion | flops 4976640 | bytes 13271045 | tf_op jit(solution)/shard_map/while/body/eval_jaxpr/add | solution.py:58
  431.4 16.0 %fusion.45 = f32[1,829440]{1,0:T(1,128)} fusion(f32[1,829440]{1,0:T(1,128)} %get-tuple-element.182, pred[]{:T(512)S(6)} %compare.15, f32[1,829440]{1,0:T(1,128)} %get-tuple-element.190, f32[8,829440]{1,0:T(8,128)} %get-tuple-element.189, s32[]{:T(128)} %get-tuple-element.181), kind=kLoop, calls=%fused_computation.1.clone.1 | loop fusion | flops 4976640 | bytes 13271045 | tf_op jit(solution)/shard_map/while/body/eval_jaxpr/add | solution.py:58
  447.3 16.0 %fusion.45 = f32[1,829440]{1,0:T(1,128)} fusion(f32[1,829440]{1,0:T(1,128)} %get-tuple-element.182, pred[]{:T(512)S(6)} %compare.15, f32[1,829440]{1,0:T(1,128)} %get-tuple-element.190, f32[8,829440]{1,0:T(8,128)} %get-tuple-element.189, s32[]{:T(128)} %get-tuple-element.181), kind=kLoop, calls=%fused_computation.1.clone.1 | loop fusion | flops 4976640 | bytes 13271045 | tf_op jit(solution)/shard_map/while/body/eval_jaxpr/add | solution.py:58
  463.3 16.0 %fusion.45 = f32[1,829440]{1,0:T(1,128)} fusion(f32[1,829440]{1,0:T(1,128)} %get-tuple-element.182, pred[]{:T(512)S(6)} %compare.15, f32[1,829440]{1,0:T(1,128)} %get-tuple-element.190, f32[8,829440]{1,0:T(8,128)} %get-tuple-element.189, s32[]{:T(128)} %get-tuple-element.181), kind=kLoop, calls=%fused_computation.1.clone.1 | loop fusion | flops 4976640 | bytes 13271045 | tf_op jit(solution)/shard_map/while/body/eval_jaxpr/add | solution.py:58
  479.2 16.0 %fusion.45 = f32[1,829440]{1,0:T(1,128)} fusion(f32[1,829440]{1,0:T(1,128)} %get-tuple-element.182, pred[]{:T(512)S(6)} %compare.15, f32[1,829440]{1,0:T(1,128)} %get-tuple-element.190, f32[8,829440]{1,0:T(8,128)} %get-tuple-element.189, s32[]{:T(128)} %get-tuple-element.181), kind=kLoop, calls=%fused_computation.1.clone.1 | loop fusion | flops 4976640 | bytes 13271045 | tf_op jit(solution)/shard_map/while/body/eval_jaxpr/add | solution.py:58
  495.2 37.4 %subtract_reduce_fusion = f32[829440]{0:T(1024)} fusion(f32[1,829440]{1,0:T(1,128)} %get-tuple-element.105, f32[1,829440]{1,0:T(1,128)} %get-tuple-element.195, f32[1,829440]{1,0:T(1,128)} %broadcast_in_dim_reshape.3), kind=kLoop, calls=%fused_computation.37 | loop fusion | flops 4976640 | bytes 13271040 | tf_op jit(solution)/shard_map/sub | solution.py:89
  553.8 23.7 %fusion.37 = (bf16[1,9,32,26496]{3,2,1,0:T(8,128)(2,1)}, f32[1,9,32,26496]{3,2,1,0:T(8,128)}) fusion(bf16[9,9,32,32]{3,1,0,2:T(8,128)(2,1)S(1)} %copy-done.3, bf16[9,1,32,26496]{3,2,0,1:T(8,128)(2,1)} %bitcast_dynamic-update-slice_fusion.8), kind=kOutput, calls=%fused_computation.83 | convolution fusion | flops 4402999296 | bytes 61212672 | tf_op jit(solution)/shard_map/dkir,dmix->mkrx/dot_general | solution.py:101
  579.9 12.4 %copy.120 = bf16[1,384,11520]{1,2,0:T(8,128)(2,1)} copy(bf16[1,384,11520]{2,1,0:T(8,128)(2,1)} %param.13) | data formatting | bytes 17694720 | tf_op args[0]
  592.3 24.6 %slice.209 = f32[1,9,32,25920]{3,2,1,0:T(8,128)} slice(f32[1,9,32,26496]{3,2,1,0:T(8,128)} %get-tuple-element.149), slice={[0:1], [0:9], [0:32], [288:26208]} | slice | bytes 59719680 | tf_op jit(solution)/shard_map/slice | solution.py:106
  628.7 16.5 %convert_element_type.58 = bf16[1,9,32,25920]{3,2,1,0:T(8,128)(2,1)} convert(f32[1,9,32,25920]{3,2,1,0:T(8,128)} %scatter-add.9) | non-fusion elementwise | flops 7464960 | bytes 44789760 | tf_op jit(solution)/shard_map/convert_element_type | solution.py:109
  645.2 39.2 %reshape.252 = bf16[9,32,360,72]{3,2,1,0:T(8,128)(2,1)} reshape(bf16[1,9,32,25920]{3,2,1,0:T(8,128)(2,1)} %convert_element_type.58) | data formatting | bytes 29859840 | tf_op jit(solution)/shard_map/reshape.105
  684.4 31.7 %copy.119 = bf16[9,72,360,32]{2,3,1,0:T(8,128)(2,1)} copy(bf16[9,72,360,32]{1,2,3,0:T(8,128)(2,1)} %bitcast.185) | data formatting | bytes 29859840 | tf_op jit(solution)/shard_map/mkrjo,mcjr->koc/dot_general | solution.py:115
  716.1 26.0 %copy.121 = bf16[648,360,32]{0,2,1:T(8,128)(2,1)} copy(bf16[648,360,32]{1,2,0:T(8,128)(2,1)} %bitcast.187) | data formatting | bytes 29859840 | tf_op jit(solution)/shard_map/mkrjo,mcjr->koc/dot_general | solution.py:115
  742.1 14.1 %convolution_bitcast_fusion.10 = f32[648,384]{1,0:T(8,128)} fusion(bf16[648,360,32]{0,2,1:T(8,128)(2,1)} %copy.121, bf16[384,360,32]{0,2,1:T(8,128)(2,1)} %bitcast.188), kind=kOutput, calls=%fused_computation.51 | convolution fusion | flops 5733089280 | bytes 24772608 | tf_op jit(solution)/shard_map/mkrjo,mcjr->koc/dot_general | solution.py:115
  756.2 17.3 %fusion.11 = bf16[1,384,360,32]{1,2,3,0:T(8,128)(2,1)} fusion(bf16[9,32,360,72]{3,2,1,0:T(8,128)(2,1)} %reshape.252, bf16[9,72,384,1]{2,1,3,0:T(8,128)(2,1)S(1)} %bitcast.184), kind=kOutput, calls=%fused_computation.35 | convolution fusion | flops 5737512960 | bytes 24274944 | tf_op jit(solution)/shard_map/koc,mkrjo->mcjr/dot_general | solution.py:110
  781.7 12.4 %copy.122 = bf16[1,384,11520]{2,1,0:T(8,128)(2,1)} copy(bf16[1,384,11520]{1,2,0:T(8,128)(2,1)} %bitcast.189) | data formatting | bytes 17694720
  794.0 93.0 %all-reduce.3.cloned.1.call-done = f32[648,384]{1,0:T(8,128)} async-done(((f32[648,384]{1,0:T(8,128)}), f32[648,384]{1,0:T(8,128)}) %all-reduce.3.cloned.1.call-update) | async-done | bytes 995344 | tf_op jit(solution)/shard_map/psum | solution.py:120
  (61 shorter events, 132.9 us)
Async XLA Ops:
  7.2 30.7 %copy-start = (bf16[648,384]{1,0:T(8,128)(2,1)S(1)}, bf16[648,384]{1,0:T(8,128)(2,1)}, u32[]{:S(2)}) copy-start(bf16[648,384]{1,0:T(8,128)(2,1)} %param.14) | copy-start | bytes 1492996
  7.2 338.9 %all-gather.3.cloned.1.call-start = ((), (), s32[]{:S(2)}) async-start(), calls=%async_computation.1 | async-start | bytes 29859840 | tf_op jit(solution)/shard_map/all_gather | solution.py:86
  8.2 10.2 %collective-permute-start = (bf16[1,384,128]{2,1,0:T(8,128)(2,1)S(1)}, bf16[1,384,128]{2,1,0:T(8,128)(2,1)S(1)}, u32[]{:S(2)}, u32[]{:S(2)}) collective-permute-start(bf16[1,384,128]{2,1,0:T(8,128)(2,1)S(1)} %get-tuple-element.137), channel_id=1, source_target_pairs={{0,1},{1,2},{2,3},{3,0},{4,5},{5,6},{6,7},{7,4},{8,9},{9,10},{10,1... | collective-permute-start | bytes 294920 | tf_op jit(solution)/shard_map/ppermute | solution.py:24
  10.4 8.0 collective-permute-start.1
  16.5 1.0 copy-start.2
  125.8 9.7 %copy-start.1 = (bf16[1,9,32,26496]{3,2,1,0:T(8,128)(2,1)S(1)}, bf16[1,9,32,26496]{3,2,1,0:T(8,128)(2,1)}, u32[]{:S(2)}) copy-start(bf16[1,9,32,26496]{3,2,1,0:T(8,128)(2,1)} %reshape.238) | copy-start | bytes 45785092
  182.3 12.7 %copy-start.4 = (bf16[9,32,32]{2,0,1:T(8,128)(2,1)S(1)}, bf16[9,32,32]{2,0,1:T(8,128)(2,1)}, u32[]{:S(2)}) copy-start(bf16[9,32,32]{2,0,1:T(8,128)(2,1)} %get-tuple-element.139) | copy-start | bytes 55300
  182.3 12.7 %copy-start.6 = (f32[25920,32]{0,1:T(8,128)S(1)}, f32[25920,32]{0,1:T(8,128)}, u32[]{:S(2)}) copy-start(f32[25920,32]{0,1:T(8,128)} %convolution_bitcast_fusion.1) | copy-start | bytes 9953284
  214.7 672.4 %all-reduce.3.cloned.1.call-start = ((), (), s32[]{:S(2)}) async-start(), calls=%async_computation | async-start | bytes 1990656 | tf_op jit(solution)/shard_map/psum | solution.py:120
  495.2 41.3 %copy-start.5 = (f32[32]{0:T(128)S(1)}, f32[32]{0:T(128)}, u32[]{:S(2)}) copy-start(f32[32]{0:T(128)} %param.19) | copy-start | bytes 388
  545.2 8.6 copy-start.3
  578.6 40.3 %collective-permute-start.2 = (bf16[1,9,32,288]{3,2,1,0:T(8,128)(2,1)S(1)}, bf16[1,9,32,288]{3,2,1,0:T(8,128)(2,1)S(1)}, u32[]{:S(2)}, u32[]{:S(2)}) collective-permute-start(bf16[1,9,32,288]{3,2,1,0:T(8,128)(2,1)S(1)} %get-tuple-element.136), channel_id=1, source_target_pairs={{0,1},{1,2},{2,3},{3,0},{4,5},{5,6},{6,7},{7,4},{8,9},{9,10},{10,1... | collective-permute-start | bytes 497672 | tf_op jit(solution)/shard_map/ppermute | solution.py:36
  616.9 7.0 collective-permute-start.3
Sparse Core Ops, SparseCore 0:
  214.8 131.2 all-gather.2
  756.3 130.6 all-reduce.2
where the time goes:
time: 912 us; the launch traced here: 896 us
  local copies, waits for them, and re-layouts  328 us (36%)
  other arithmetic  196 us (21%)
  waiting for transfers between devices  189 us (21%)
  matrix products  161 us (18%)
  between operations  14.4 us (2%)
    add x8, other arithmetic, add_member(): return total + smooth_slope(values - single)  127 us
    all_gather x1, waiting for transfers between devices, shards(): everyone = lax.all_gather(flat_out, 'ens', axis=0, tiled=True)  96 us
    psum x1, waiting for transfers between devices, shards(): lax.psum(weight_part, ('ens', 'lon'))  93 us
    dot_general x9, matrix products, shards(): jnp.einsum('kir,mkrx->mix', kernel[offset], window, preferred_element_typ...  80 us
    unnamed x28, local copies, waits for them, and re-layouts  76.9 us
    dot_general x2, local copies, waits for them, and re-layouts, shards(): jnp.einsum('mkrjo,mcjr->koc', grad_local, feature_cells, preferred_elemen...  57.7 us
    reshape x1, local copies, waits for them, and re-layouts, shards(): projected = projected.reshape(mem_dev, K, LAT, (lon_dev + 2 * R) * O)  39.8 us
    another operation x1, local copies, waits for them, and re-layouts  39.2 us
  transfers between devices with their start and end apart: 6, of which 2 were waited for; matrix products, arithmetic and copies ran while one was open for 13% of the time, Pallas kernels for 0%

commit v1 on v0

v1 whole, which is shorter than its diff:
```python
import functools
import math

import jax
import jax.numpy as jnp
from jax import lax
from jax.experimental import pallas as pl
from jax.experimental.pallas import tpu as pltpu
from jax.sharding import PartitionSpec as P

O = 72
OP = 80
K = 9
R = 4
LAT = 32
SMOOTH = 0.25
BLK = 256
HALF = 128
F32 = jnp.float32
BF16 = jnp.bfloat16
MESH = pl.DeviceIdType.MESH
VMEM_LIMIT = 60 * 1024 * 1024


def whole(shape):
    return pl.BlockSpec(shape, lambda s: (0,) * len(shape))


def kernel_rows(basis_vals, row_of, col_off):
    code = (col_off + R) * LAT + row_of
    ids = jnp.arange((2 * R + 1) * LAT, dtype=jnp.int32)
    hit = (code[:, :, None] == ids[None, None, :]).astype(F32)
    table = jnp.einsum("isk,isq->ikq", basis_vals, hit, precision=lax.Precision.HIGHEST)
    return table.astype(BF16)


def band_tables(table):
    taps = 2 * R + 1
    cols = BLK // LAT
    four = table.reshape(LAT, K, taps, LAT)
    ahead = four.transpose(1, 2, 3, 0)
    back = four[:, :, ::-1].transpose(1, 2, 0, 3)
    out = []
    for base in (ahead, back):
        parts = [
            jnp.pad(base, ((0, 0), (j, 2 * cols - taps - j), (0, 0), (0, 0))).reshape(
                K, 2 * BLK, LAT
            )
            for j in range(cols)
        ]
        out.append(jnp.concatenate(parts, axis=2))
    return out


def forward_kernel(group, steps, feat, left, right, weight, band, out, proj):
    s = pl.program_id(0)

    def put(values, h, lo):
        for k in range(K):
            proj[k, h, :, lo : lo + HALF] = values[k * OP : (k + 1) * OP].astype(BF16)

    @pl.when(s == 0)
    def _():
        put(jnp.dot(weight[...], left[...], preferred_element_type=F32), 0, 0)

    @pl.when(s < steps)
    def _():
        def one(n, carry):
            lanes = pl.ds(pl.multiple_of(n * BLK, BLK), BLK)
            got = jnp.dot(weight[...], feat[:, lanes], preferred_element_type=F32)
            h = s * group + n
            put(got[:, :HALF], h, HALF)
            put(got[:, HALF:], h + 1, 0)
            return carry

        lax.fori_loop(0, group, one, 0)

    @pl.when(s == steps)
    def _():
        put(jnp.dot(weight[...], right[...], preferred_element_type=F32), steps * group, HALF)

    @pl.when(s > 0)
    def _():
        g0 = (s - 1) * group
        acc = jnp.zeros((group * OP, BLK), F32)
        for k in range(K):
            for part in range(2):
                lhs = proj[k, pl.ds(g0 + part, group)].reshape(group * OP, BLK)
                acc = acc + jnp.dot(
                    lhs, band[k, part * BLK : (part + 1) * BLK, :], preferred_element_type=F32
                )
        for g in range(group):
            piece = acc[g * OP : g * OP + O]
            both = jnp.concatenate([piece[:, :HALF], piece[:, HALF:]], axis=0)
            out[g * 2 * O : (g + 1) * 2 * O, :] = both.astype(BF16)


def forward(feat, left, right, weight, band, group, steps, rows):
    chan = feat.shape[0]
    wide = group * BLK
    return pl.pallas_call(
        functools.partial(forward_kernel, group, steps),
        out_shape=jax.ShapeDtypeStruct((rows, HALF), BF16),
        grid=(steps + 1,),
        in_specs=[
            pl.BlockSpec((chan, wide), lambda s: (0, jnp.minimum(s, steps - 1))),
            whole(left.shape),
            whole(right.shape),
            whole(weight.shape),
            whole(band.shape),
        ],
        out_specs=pl.BlockSpec((group * 2 * O, HALF), lambda s: (jnp.maximum(s - 1, 0), 0)),
        scratch_shapes=[pltpu.VMEM((K, steps * group + 1, OP, BLK), BF16)],
        compiler_params=pltpu.CompilerParams(vmem_limit_bytes=VMEM_LIMIT),
        name="forward_conv",
    )(feat, left, right, weight, band)


def greet(peers):
    barrier = pltpu.get_barrier_semaphore()
    for peer in peers:
        pl.semaphore_signal(barrier, inc=1, device_id=peer, device_id_type=MESH)
    pl.semaphore_wait(barrier, len(peers))


def slope_kernel(n, dec, obs, lat, cot, recv, send, ssem1, rsem1, ssem2, rsem2):
    me = lax.axis_index("ens")
    rows = obs.shape[0]
    greet([{"ens": lax.rem(me + off, n)} for off in range(1, n)])
    first = []
    for off in range(1, n):
        peer = lax.rem(me + off, n)
        copy = pltpu.make_async_remote_copy(
            src_ref=dec.at[pl.ds(pl.multiple_of(peer * rows, 16), rows)],
            dst_ref=recv.at[off],
            send_sem=ssem1.at[off],
            recv_sem=rsem1.at[off],
            device_id={"ens": peer},
            device_id_type=MESH,
        )
        copy.start()
        first.append(copy)
    for copy in first:
        copy.wait()
    own = pl.multiple_of(me * rows, 16)
    lat_row = jnp.broadcast_to(lat[0:1, :], (16, HALF))

    def smooth(diff):
        return diff * lax.rsqrt(diff * diff + SMOOTH * SMOOTH)

    def one(step, carry):
        at = pl.multiple_of(step * 16, 16)
        values = [dec[pl.ds(pl.multiple_of(own + at, 16), 16), :].astype(F32)]
        values += [recv[off, pl.ds(at, 16), :].astype(F32) for off in range(1, n)]
        sums = [None] * n
        for a in range(n):
            for b in range(a + 1, n):
                pair = smooth(values[a] - values[b])
                sums[a] = pair if sums[a] is None else sums[a] + pair
                sums[b] = -pair if sums[b] is None else sums[b] - pair
        target = obs[pl.ds(at, 16), :]
        for a in range(n):
            slope = smooth(values[a] - target) - sums[a] * (1.0 / (n - 1))
            result = (slope * lat_row).astype(BF16)
            if a == 0:
                cot[pl.ds(pl.multiple_of(own + at, 16), 16), :] = result
            else:
                send[a, pl.ds(at, 16), :] = result
        return carry

    lax.fori_loop(0, rows // 16, one, 0)
    second = []
    for off in range(1, n):
        peer = lax.rem(me - off + n, n)
        copy = pltpu.make_async_remote_copy(
            src_ref=send.at[off],
            dst_ref=cot.at[pl.ds(own, rows)],
            send_sem=ssem2.at[off],
            recv_sem=rsem2.at[off],
            device_id={"ens": peer},
            device_id_type=MESH,
        )
        copy.start()
        second.append(copy)
    for copy in second:
        copy.wait()


def slopes(n, dec, obs, lat):
    rows = obs.shape[0]
    vmem = pl.BlockSpec(memory_space=pltpu.VMEM)
    return pl.pallas_call(
        functools.partial(slope_kernel, n),
        out_shape=jax.ShapeDtypeStruct(dec.shape, BF16),
        in_specs=[vmem] * 3,
        out_specs=vmem,
        scratch_shapes=[
            pltpu.VMEM((n, rows, HALF), BF16),
            pltpu.VMEM((n, rows, HALF), BF16),
            pltpu.SemaphoreType.DMA((n,)),
            pltpu.SemaphoreType.DMA((n,)),
            pltpu.SemaphoreType.DMA((n,)),
            pltpu.SemaphoreType.DMA((n,)),
        ],
        compiler_params=pltpu.CompilerParams(
            collective_id=0, has_side_effects=True, vmem_limit_bytes=VMEM_LIMIT
        ),
        name="member_slopes",
    )(dec, obs, lat)


WG_ROWS = 2048
WG_PART = 656


def backward_kernel(
    group, steps, cells, padded, cot, left, right, weight_t, band, feat, grad, wgrad, ext, spread, acc
):
    s = pl.program_id(0)
    blocks = steps * group

    @pl.when(s == 0)
    def _():
        ext[:, O:, :] = jnp.zeros((blocks + 1, OP - O, BLK), BF16)
        ext[0, :O, :HALF] = left[...]
        ext[blocks, :O, HALF:] = right[...]

        def one(b, carry):
            pair = cot[pl.ds(pl.multiple_of(b * 2 * O, 16), 2 * O), :].astype(F32)
            ext[b, :O, HALF:] = pair[:O].astype(BF16)
            ext[b + 1, :O, :HALF] = pair[O:].astype(BF16)
            return carry

        lax.fori_loop(0, blocks, one, 0)
        acc[...] = jnp.zeros_like(acc)

    g0 = s * group
    for k in range(K):
        got = jnp.zeros((group * OP, BLK), F32)
        for part in range(2):
            lhs = ext[pl.ds(g0 + part, group)].reshape(group * OP, BLK)
            got = got + jnp.dot(
                lhs, band[k, part * BLK : (part + 1) * BLK, :], preferred_element_type=F32
            )
        if padded:
            row = lax.broadcasted_iota(jnp.int32, got.shape, 0) // OP
            lane = lax.broadcasted_iota(jnp.int32, got.shape, 1)
            got = jnp.where((g0 + row) * BLK + lane < cells, got, 0.0)
        got = got.astype(BF16)
        for g in range(group):
            spread[k * OP : (k + 1) * OP, g * BLK : (g + 1) * BLK] = got[g * OP : (g + 1) * OP]

    acc[...] += lax.dot_general(
        spread[...], feat[...], (((1,), (1,)), ((), ())), preferred_element_type=F32
    )

    def one_grad(n, carry):
        lanes = pl.ds(pl.multiple_of(n * BLK, BLK), BLK)
        grad[:, lanes] = jnp.dot(
            weight_t[...], spread[:, lanes], preferred_element_type=F32
        ).astype(BF16)
        return carry

    lax.fori_loop(0, group, one_grad, 0)

    @pl.when(s == steps - 1)
    def _():
        parts = acc.shape[1] // HALF
        wgrad[parts * WG_PART - 16 :, :] = jnp.zeros((WG_ROWS - parts * WG_PART + 16, HALF), BF16)
        for t in range(parts):
            rows = [
                acc[k * OP : k * OP + O, t * HALF : (t + 1) * HALF] for k in range(K)
            ] + [jnp.zeros((8, HALF), F32)]
            wgrad[t * WG_PART : (t + 1) * WG_PART, :] = jnp.concatenate(rows, axis=0).astype(BF16)


def backward(cot, left, right, weight_t, band, feat, group, steps, cells):
    chan = feat.shape[0]
    wide = group * BLK
    blocks = steps * group
    return pl.pallas_call(
        functools.partial(backward_kernel, group, steps, cells, cells != blocks * BLK),
        out_shape=(
            jax.ShapeDtypeStruct(feat.shape, BF16),
            jax.ShapeDtypeStruct((WG_ROWS, HALF), BF16),
        ),
        grid=(steps,),
        in_specs=[
            whole(cot.shape),
            whole(left.shape),
            whole(right.shape),
            whole(weight_t.shape),
            whole(band.shape),
            pl.BlockSpec((chan, wide), lambda s: (0, s)),
        ],
        out_specs=(pl.BlockSpec((chan, wide), lambda s: (0, s)), whole((WG_ROWS, HALF))),
        scratch_shapes=[
            pltpu.VMEM((blocks + 1, OP, BLK), BF16),
            pltpu.VMEM((K * OP, wide), BF16),
            pltpu.VMEM((K * OP, chan), F32),
        ],
        compiler_params=pltpu.CompilerParams(vmem_limit_bytes=VMEM_LIMIT),
        name="backward_conv",
    )(cot, left, right, weight_t, band, feat)


def reduce_kernel(ne, nl, scale, part, out, recv1, mid, recv2, got, *sems):
    (ss1, rs1, ss2, rs2, ss3, rs3, ss4, rs4) = sems
    me = lax.axis_index("ens")
    at = lax.axis_index("lon")
    rows = WG_ROWS // ne
    small = rows // nl
    ens_peers = [{"ens": lax.rem(me + off, ne)} for off in range(1, ne)]
    lon_peers = [{"lon": lax.rem(at + off, nl)} for off in range(1, nl)]
    greet(ens_peers + lon_peers)

    def run(copies):
        for copy in copies:
            copy.start()
        for copy in copies:
            copy.wait()

    def send(src, dst, ssem, rsem, peer):
        return pltpu.make_async_remote_copy(
            src_ref=src, dst_ref=dst, send_sem=ssem, recv_sem=rsem, device_id=peer, device_id_type=MESH
        )

    own = pl.multiple_of(me * rows, 16)
    mine = pl.multiple_of(at * small, 8)
    run(
        [
            send(
                part.at[pl.ds(pl.multiple_of(lax.rem(me + off, ne) * rows, 16), rows)],
                recv1.at[off],
                ss1.at[off],
                rs1.at[off],
                {"ens": lax.rem(me + off, ne)},
            )
            for off in range(1, ne)
        ]
    )
    total = part[pl.ds(own, rows), :].astype(F32)
    for off in range(1, ne):
        total = total + recv1[off].astype(F32)
    mid[...] = total
    run(
        [
            send(
                mid.at[pl.ds(pl.multiple_of(lax.rem(at + off, nl) * small, 8), small)],
                recv2.at[off],
                ss2.at[off],
                rs2.at[off],
                {"lon": lax.rem(at + off, nl)},
            )
            for off in range(1, nl)
        ]
    )
    total = mid[pl.ds(mine, small), :]
    for off in range(1, nl):
        total = total + recv2[off]
    recv2[0] = total
    gat = got[1]
    gat[pl.ds(mine, small), :] = total
    run(
        [
            send(
                recv2.at[0],
                gat.at[pl.ds(mine, small)],
                ss3.at[off],
                rs3.at[off],
                {"lon": lax.rem(at + off, nl)},
            )
            for off in range(1, nl)
        ]
    )
    full = got[0]
    full[pl.ds(own, rows), :] = gat[...].astype(BF16)
    run(
        [
            send(
                full.at[pl.ds(own, rows)],
                full.at[pl.ds(own, rows)],
                ss4.at[off],
                rs4.at[off],
                {"ens": lax.rem(me + off, ne)},
            )
            for off in range(1, ne)
        ]
    )
    for t in range(out.shape[1] // HALF):
        piece = full[t * WG_PART : (t + 1) * WG_PART, :].astype(F32) * scale
        out[:, t * HALF : (t + 1) * HALF] = piece[: K * O]


def reduced(ne, nl, scale, part, chan):
    vmem = pl.BlockSpec(memory_space=pltpu.VMEM)
    rows = WG_ROWS // ne
    small = rows // nl

    def body(part, out, recv1, mid, recv2, full, gat, *sems):
        reduce_kernel(ne, nl, scale, part, out, recv1, mid, recv2, (full, gat), *sems)

    return pl.pallas_call(
        body,
        out_shape=jax.ShapeDtypeStruct((K * O, chan), F32),
        in_specs=[vmem],
        out_specs=vmem,
        scratch_shapes=[
            pltpu.VMEM((ne, rows, HALF), BF16),
            pltpu.VMEM((rows, HALF), F32),
            pltpu.VMEM((nl, small, HALF), F32),
            pltpu.VMEM((WG_ROWS, HALF), BF16),
            pltpu.VMEM((rows, HALF), F32),
        ]
        + [pltpu.SemaphoreType.DMA((n,)) for n in (ne, ne, nl, nl, nl, nl, ne, ne)],
        compiler_params=pltpu.CompilerParams(
            collective_id=1, has_side_effects=True, vmem_limit_bytes=VMEM_LIMIT
        ),
        name="weight_reduce",
    )(part)


def passed_along(value, axis, steps):
    count = lax.axis_size(axis)
    return lax.ppermute(value, axis, [(i, (i + steps) % count) for i in range(count)])


def shards(features, proj_weight, basis_vals, row_of, col_off, observed, lat_weight):
    ne = lax.axis_size("ens")
    nl = lax.axis_size("lon")
    assert features.shape[0] == 1
    feat = features[0]
    chan, cells = feat.shape
    aligned = cells % BLK == 0
    blocks = cells // BLK if aligned else pl.cdiv(cells + HALF, BLK)
    group = max(g for g in range(1, 10) if blocks % g == 0)
    steps = blocks // group
    tiles = 2 * blocks
    per = pl.cdiv(tiles, ne)
    per += per % 2
    rows = per * ne * O
    extra = blocks * BLK - cells

    left = passed_along(feat[:, cells - HALF :], "lon", 1)
    right = passed_along(feat[:, :HALF], "lon", -1)
    ahead, back = band_tables(kernel_rows(basis_vals, row_of, col_off))
    weight = jnp.pad(proj_weight.reshape(K, O, chan), ((0, 0), (0, OP - O), (0, 0)))
    weight = weight.reshape(K * OP, chan)
    if not aligned:
        feat = jnp.pad(jnp.concatenate([feat, right], axis=1), ((0, 0), (0, extra - HALF)))
        right = jnp.zeros_like(right)
    dec = forward(feat, left, right, weight, ahead, group, steps, rows)

    obs = jnp.pad(observed, ((0, 0), (0, per * ne * HALF - cells)))
    obs = lax.dynamic_slice_in_dim(obs, lax.axis_index("ens") * per * HALF, per * HALF, axis=1)
    obs = obs.reshape(O, per, HALF).transpose(1, 0, 2).reshape(per * O, HALF)
    lat = jnp.broadcast_to(jnp.tile(lat_weight, HALF // LAT)[None, :], (8, HALF))
    cot = slopes(ne, dec, obs, lat)

    if aligned:
        cot_left = passed_along(cot[(tiles - 1) * O : tiles * O], "lon", 1)
        cot_right = passed_along(cot[:O], "lon", -1)
    else:
        flat = cot.reshape(per * ne, O, HALF).transpose(1, 0, 2).reshape(O, per * ne * HALF)
        flat = flat[:, :cells]
        cot_left = passed_along(flat[:, cells - HALF :], "lon", 1)
        cot_right = passed_along(flat[:, :HALF], "lon", -1)
        flat = jnp.pad(
            jnp.concatenate([flat, cot_right], axis=1),
            ((0, 0), (0, per * ne * HALF - cells - HALF)),
        )
        cot = flat.reshape(O, per * ne, HALF).transpose(1, 0, 2).reshape(rows, HALF)
        cot_right = jnp.zeros_like(cot_right)
    grad, part = backward(cot, cot_left, cot_right, weight.T, back, feat, group, steps, cells)
    scale = 1.0 / math.sqrt(ne * (cells // LAT) * nl * LAT)
    weight_grad = reduced(ne, nl, scale, part, chan)
    return (grad[:, :cells][None], weight_grad)


def solution(mesh):
    in_specs = (P("ens", None, "lon"), P(), P(), P(), P(), P(None, "lon"), P())
    out_specs = (P("ens", None, "lon"), P())
    return jax.shard_map(shards, mesh=mesh, in_specs=in_specs, out_specs=out_specs, check_vma=False)
```

time: 912 us -> 206 us (0.23); the launches traced: 896 us -> 205 us
  local copies, waits for them, and re-layouts: 328 us -> 48.3 us
  other arithmetic: 196 us -> 0.74 us
  waiting for transfers between devices: 189 us -> 0.01 us
  matrix products: 161 us -> 0.78 us
  Pallas kernels: 0 us -> 147 us
  between operations: 14.4 us -> 0.73 us
    dot_general x14 -> x1, matrix products: 161 us -> 0.78 us  [kernel_rows(): jnp.einsum('isk,isq->ikq', basis_vals, hit, precision=lax.Precision.HIGHEST)]
    pallas_call x0 -> x4, Pallas kernels: none -> 147 us  [the longest x1 50.3 us: slopes(): pl.pallas_call(functools.partial(slope_kernel, n), out_shape=jax.ShapeDty...]
    add x10 -> x1, other arithmetic: 129 us -> 0.74 us  [kernel_rows(): code = (col_off + R) * LAT + row_of]
    all_gather x1 -> x0, waiting for transfers between devices: 96 us -> none  [shards(): everyone = lax.all_gather(flat_out, 'ens', axis=0, tiled=True)]
    psum x1 -> x0, waiting for transfers between devices: 93 us -> none  [shards(): lax.psum(weight_part, ('ens', 'lon'))]
    unnamed x28 -> x18, local copies, waits for them, and re-layouts: 76.9 us -> 5.75 us
    dot_general x2 -> x0, local copies, waits for them, and re-layouts: 57.7 us -> none  [shards(): jnp.einsum('mkrjo,mcjr->koc', grad_local, feature_cells, preferred_elemen...]
    another operation x3 -> x1, local copies, waits for them, and re-layouts: 52.9 us -> 0.01 us  [shards(): jnp.tile(lat_weight, HALF // LAT)[None, :]]
  transfers between devices with their start and end apart: 6 -> 4, of which waited for: 2 -> 0; matrix products, arithmetic and copies ran while one was open for 13% -> 21% of each run, Pallas kernels for 0% -> 0%
where the time goes in v1:
time: 206 us; the launch traced here: 205 us
  Pallas kernels  147 us (71%)
  local copies, waits for them, and re-layouts  48.3 us (23%)
  starting transfers between devices  7.4 us (4%)
    pallas_call x1, Pallas kernels, slopes(): pl.pallas_call(functools.partial(slope_kernel, n), out_shape=jax.ShapeDty...  50.3 us
    pallas_call x1, Pallas kernels, backward(): pl.pallas_call(functools.partial(backward_kernel, group, steps, cells, ce...  38.4 us
    pallas_call x1, Pallas kernels, forward(): pl.pallas_call(functools.partial(forward_kernel, group, steps), out_shape...  29.2 us
    pallas_call x1, Pallas kernels, reduced(): pl.pallas_call(body, out_shape=jax.ShapeDtypeStruct((K * O, chan), F32),...  29 us
    concatenate x2, local copies, waits for them, and re-layouts, band_tables(): out.append(jnp.concatenate(parts, axis=2))  19.8 us
    pad x2, local copies, waits for them, and re-layouts, band_tables(): jnp.pad(base, ((0, 0), (j, 2 * cols - taps - j), (0, 0), (0, 0)))  10.8 us
    ppermute x4, starting transfers between devices, passed_along(): lax.ppermute(value, axis, [(i, (i + steps) % count) for i in range(count)])  7.4 us
    unnamed x18, local copies, waits for them, and re-layouts  5.75 us
  transfers between devices with their start and end apart: 4, of which 0 were waited for; matrix products, arithmetic and copies ran while one was open for 21% of the time, Pallas kernels for 0%

profile of v1, /device:TPU:1, one launch (start us, length us, event | category | flops | bytes accessed | tf_op | source)
XLA Modules:
  0.0 204.9 jit_solution(11538623871436570552)
XLA Ops:
  0.6 0.0 copy-start
  0.6 1.6 fusion.5
  2.3 2.1 %collective-permute-start = (bf16[384,128]{1,0:T(8,128)(2,1)}, bf16[384,128]{1,0:T(8,128)(2,1)S(1)}, u32[]{:S(2)}, u32[]{:S(2)}) collective-permute-start(bf16[384,128]{1,0:T(8,128)(2,1)} %get-tuple-element.7), channel_id=1, source_target_pairs={{0,1},{1,2},{2,3},{3,0},{4,5},{5,6},{6,7},{7,4},{8,9},{9,10},{10,1... | collective-permute-start | bytes 294920 | tf_op jit(solution)/shard_map/ppermute | solution.py:425
  4.4 2.0 collective-permute-start.1
  6.4 0.7 multiply_add_fusion
  7.2 0.8 fusion.2
  7.9 0.4 copy.15
  8.3 4.0 %fusion.8 = (bf16[9,16,32,32]{3,2,1,0:T(8,128)(2,1)S(1)}, bf16[9,16,32,32]{3,2,1,0:T(8,128)(2,1)S(1)}, bf16[9,16,32,32]{3,2,1,0:T(8,128)(2,1)}, bf16[9,16,32,32]...) fusion(bf16[9,9,32,32]{3,2,1,0:T(8,128)(2,1)S(1)} %bitcast.33), kind=kLoop, calls=%fused_computation.12 | loop fusion | bytes 2525184 | tf_op jit(solution)/shard_map/jit(_pad)/pad | solution.py:46
  12.4 1.8 pad_dynamic-slice_fusion
  14.2 1.9 reshape.81
  16.1 2.0 copy.16
  18.1 0.1 broadcast_in_dim.12
  18.1 0.9 reverse_bitcast_fusion
  19.0 2.3 %copy.26 = bf16[9,9,32,32]{3,2,1,0:T(8,128)(2,1)} copy(bf16[9,9,32,32]{2,3,1,0:T(8,128)(2,1)} %reverse_bitcast_fusion) | data formatting | bytes 331776
  21.3 0.9 pad.64
  22.2 9.9 %concatenate.6.band = bf16[9,512,256]{2,1,0:T(8,128)(2,1)} concatenate(bf16[9,512,32]{2,1,0:T(8,128)(2,1)} %bitcast.44, bf16[9,512,32]{2,1,0:T(8,128)(2,1)} %bitcast.43, bf16[9,512,32]{2,1,0:T(8,128)(2,1)} %bitcast.42, bf16[9,512,32]{2,1,0:T(8,128)(2,1)} %bitcast.41, bf16[9,512,32]{2,1,0:T(8,128)(2,1)} %bitcast.40, bf16[9,512,32]{2,1,0:T(8,128)(2,1)} %bitcast.39, ...), dimensions={2} | concatenate | bytes 4718592 | tf_op jit(solution)/shard_map/concatenate | solution.py:51
  32.1 0.0 collective-permute-done.1.right
  32.1 0.6 copy-done.3
  32.7 0.0 copy-done.4
  32.8 29.2 %forward_conv.1.dec = bf16[6912,128]{1,0:T(8,128)(2,1)} custom-call(bf16[384,11520]{1,0:T(8,128)(2,1)} %bitcast.31, bf16[384,128]{1,0:T(8,128)(2,1)} %copy-done.3, bf16[384,128]{1,0:T(8,128)(2,1)} %copy-done.4, bf16[720,384]{1,0:T(8,128)(2,1)} %bitcast.35, bf16[9,512,256]{2,1,0:T(8,128)(2,1)} %concatenate.6.band), custom_call_target="tpu_custom_call" | custom-call | tf_op jit(solution)/shard_map/forward_conv/pallas_call | solution.py:101
  62.0 0.6 broadcast_in_dim.13.lat
  62.6 50.3 %member_slopes.1.cot = bf16[6912,128]{1,0:T(8,128)(2,1)} custom-call(bf16[6912,128]{1,0:T(8,128)(2,1)} %forward_conv.1.dec, f32[864,128]{1,0:T(8,128)} %bitcast.55, f32[8,128]{1,0:T(8,128)} %broadcast_in_dim.13.lat), custom_call_target="tpu_custom_call" | custom-call | tf_op jit(solution)/shard_map/member_slopes/pallas_call | solution.py:192
  112.9 0.7 fusion.6
  113.6 3.3 %collective-permute-start.3 = (bf16[72,128]{1,0:T(8,128)(2,1)S(1)}, bf16[72,128]{1,0:T(8,128)(2,1)S(1)}, u32[]{:S(2)}, u32[]{:S(2)}) collective-permute-start(bf16[72,128]{1,0:T(8,128)(2,1)S(1)} %get-tuple-element.8), channel_id=1, source_target_pairs={{0,3},{1,0},{2,1},{3,2},{4,7},{5,4},{6,5},{7,6},{8,11},{9,8},{10,9... | collective-permute-start | bytes 55304 | tf_op jit(solution)/shard_map/ppermute | solution.py:425
  116.9 6.7 %fusion.7 = (bf16[9,16,32,32]{3,2,1,0:T(8,128)(2,1)S(1)}, bf16[9,16,32,32]{3,2,1,0:T(8,128)(2,1)S(1)}, bf16[9,16,32,32]{3,2,1,0:T(8,128)(2,1)}, bf16[9,16,32,32]...) fusion(bf16[9,9,32,32]{3,2,1,0:T(8,128)(2,1)} %copy.26), kind=kLoop, calls=%fused_computation.11 | loop fusion | bytes 2525184 | tf_op jit(solution)/shard_map/jit(_pad)/pad | solution.py:46
  123.6 1.1 copy.17
  124.7 9.9 %concatenate.7.band = bf16[9,512,256]{2,1,0:T(8,128)(2,1)} concatenate(bf16[9,512,32]{2,1,0:T(8,128)(2,1)} %bitcast.52, bf16[9,512,32]{2,1,0:T(8,128)(2,1)} %bitcast.51, bf16[9,512,32]{2,1,0:T(8,128)(2,1)} %bitcast.50, bf16[9,512,32]{2,1,0:T(8,128)(2,1)} %bitcast.49, bf16[9,512,32]{2,1,0:T(8,128)(2,1)} %bitcast.48, bf16[9,512,32]{2,1,0:T(8,128)(2,1)} %bitcast.47, ...), dimensions={2} | concatenate | bytes 4718592 | tf_op jit(solution)/shard_map/concatenate | solution.py:51
  134.7 0.6 copy-done.5
  135.2 0.0 copy-done.6
  135.2 38.4 %backward_conv.1 = (bf16[384,11520]{1,0:T(8,128)(2,1)}, bf16[2048,128]{1,0:T(8,128)(2,1)}) custom-call(bf16[6912,128]{1,0:T(8,128)(2,1)} %member_slopes.1.cot, bf16[72,128]{1,0:T(8,128)(2,1)} %copy-done.5, bf16[72,128]{1,0:T(8,128)(2,1)} %copy-done.6, bf16[384,720]{1,0:T(8,128)(2,1)} %bitcast.53, bf16[9,512,256]{2,1,0:T(8,128)(2,1)} %concatenate.7.band, ...), custom_call_target="tpu_custom_call" | custom-call | tf_op jit(solution)/shard_map/backward_conv/pallas_call | solution.py:281
  173.7 29.0 %weight_reduce.1 = f32[648,384]{1,0:T(8,128)} custom-call(bf16[2048,128]{1,0:T(8,128)(2,1)} %get-tuple-element.5.part), custom_call_target="tpu_custom_call" | custom-call | tf_op jit(solution)/shard_map/weight_reduce/pallas_call | solution.py:403
  202.7 2.2 %copy.37 = f32[648,384]{1,0:T(8,128)} copy(f32[648,384]{1,0:T(8,128)} %weight_reduce.1) | data formatting | bytes 1990656
  (16 shorter events, 0.0 us)
Async XLA Ops:
  0.6 6.5 %copy-start = (f32[32,32,9]{1,0,2:T(8,128)S(1)}, f32[32,32,9]{1,0,2:T(8,128)}, u32[]{:S(2)}) copy-start(f32[32,32,9]{1,0,2:T(8,128)} %param.9) | copy-start | bytes 110596
  2.3 29.8 %collective-permute-start = (bf16[384,128]{1,0:T(8,128)(2,1)}, bf16[384,128]{1,0:T(8,128)(2,1)S(1)}, u32[]{:S(2)}, u32[]{:S(2)}) collective-permute-start(bf16[384,128]{1,0:T(8,128)(2,1)} %get-tuple-element.7), channel_id=1, source_target_pairs={{0,1},{1,2},{2,3},{3,0},{4,5},{5,6},{6,7},{7,4},{8,9},{9,10},{10,1... | collective-permute-start | bytes 294920 | tf_op jit(solution)/shard_map/ppermute | solution.py:425
  4.4 27.7 %collective-permute-start.1 = (bf16[384,128]{1,0:T(8,128)(2,1)S(1)}, bf16[384,128]{1,0:T(8,128)(2,1)S(1)}, u32[]{:S(2)}, u32[]{:S(2)}) collective-permute-start(bf16[384,128]{1,0:T(8,128)(2,1)S(1)} %get-tuple-element.6), channel_id=1, source_target_pairs={{0,3},{1,0},{2,1},{3,2},{4,7},{5,4},{6,5},{7,6},{8,11},{9,8},{10,9... | collective-permute-start | bytes 294920 | tf_op jit(solution)/shard_map/ppermute | solution.py:425
  14.2 3.9 %copy-start.7 = (f32[32]{0:T(128)S(1)}, f32[32]{0:T(128)}, u32[]{:S(2)}) copy-start(f32[32]{0:T(128)} %param.13) | copy-start | bytes 388
  19.0 2.3 %copy-start.2 = (bf16[648,384]{1,0:T(8,128)(2,1)S(1)}, bf16[648,384]{1,0:T(8,128)(2,1)}, u32[]{:S(2)}) copy-start(bf16[648,384]{1,0:T(8,128)(2,1)} %param.8) | copy-start | bytes 1492996
  32.1 0.6 copy-start.3
  32.1 0.7 copy-start.4
  113.6 21.0 %collective-permute-start.2 = (bf16[72,128]{1,0:T(8,128)(2,1)S(1)}, bf16[72,128]{1,0:T(8,128)(2,1)S(1)}, u32[]{:S(2)}, u32[]{:S(2)}) collective-permute-start(bf16[72,128]{1,0:T(8,128)(2,1)S(1)} %get-tuple-element.9), channel_id=1, source_target_pairs={{0,1},{1,2},{2,3},{3,0},{4,5},{5,6},{6,7},{7,4},{8,9},{9,10},{10,1... | collective-permute-start | bytes 55304 | tf_op jit(solution)/shard_map/ppermute | solution.py:425
  113.6 10.0 %copy-start.1 = (bf16[9,80,384]{2,1,0:T(8,128)(2,1)S(1)}, bf16[9,80,384]{2,1,0:T(8,128)(2,1)}, u32[]{:S(2)}) copy-start(bf16[9,80,384]{2,1,0:T(8,128)(2,1)} %pad.64) | copy-start | bytes 1658884
  113.6 21.0 %collective-permute-start.3 = (bf16[72,128]{1,0:T(8,128)(2,1)S(1)}, bf16[72,128]{1,0:T(8,128)(2,1)S(1)}, u32[]{:S(2)}, u32[]{:S(2)}) collective-permute-start(bf16[72,128]{1,0:T(8,128)(2,1)S(1)} %get-tuple-element.8), channel_id=1, source_target_pairs={{0,3},{1,0},{2,1},{3,2},{4,7},{5,4},{6,5},{7,6},{8,11},{9,8},{10,9... | collective-permute-start | bytes 55304 | tf_op jit(solution)/shard_map/ppermute | solution.py:425
  134.6 0.6 copy-start.5
  134.6 0.6 copy-start.6

commit v2 on v1

--- a/solution.py
+++ b/solution.py
@@ -34,26 +34,81 @@
     return table.astype(BF16)
 
 
-def band_tables(table):
+def side_tables(table):
     taps = 2 * R + 1
+    four = table.reshape(LAT, K, taps, LAT)
+    ahead = four.transpose(1, 2, 3, 0).reshape(K, taps * LAT, LAT)
+    back = four[:, :, ::-1].transpose(1, 2, 0, 3).reshape(K, taps * LAT, LAT)
+    return ahead, back
+
+
+def build_band(table, band):
+    lane = lax.broadcasted_iota(jnp.int32, (LAT, BLK), 1)
+    spread_lanes = (lane % LAT == lax.broadcasted_iota(jnp.int32, (LAT, BLK), 0)).astype(F32)
+    spread_lanes = spread_lanes.astype(BF16)
+    place = lane // LAT
     cols = BLK // LAT
-    four = table.reshape(LAT, K, taps, LAT)
-    ahead = four.transpose(1, 2, 3, 0)
-    back = four[:, :, ::-1].transpose(1, 2, 0, 3)
-    out = []
-    for base in (ahead, back):
-        parts = [
-            jnp.pad(base, ((0, 0), (j, 2 * cols - taps - j), (0, 0), (0, 0))).reshape(
-                K, 2 * BLK, LAT
-            )
-            for j in range(cols)
-        ]
-        out.append(jnp.concatenate(parts, axis=2))
-    return out
-
-
-def forward_kernel(group, steps, feat, left, right, weight, band, out, proj):
+
+    def one(k, carry):
+        tiled = jnp.dot(table[k], spread_lanes, preferred_element_type=F32)
+        for e in range(2 * cols):
+            block = jnp.zeros((LAT, BLK), F32)
+            for j in range(cols):
+                d = e - j
+                if 0 <= d <= 2 * R:
+                    block = jnp.where(place == j, tiled[d * LAT : (d + 1) * LAT], block)
+            band[k, e * LAT : (e + 1) * LAT, :] = block.astype(BF16)
+        return carry
+
+    lax.fori_loop(0, K, one, 0)
+
+
+def padded_weight(weight):
+    wide = weight[...].astype(F32)
+    gap = jnp.zeros((OP - O, wide.shape[1]), F32)
+    rows = []
+    for k in range(K):
+        rows += [wide[k * O : (k + 1) * O], gap]
+    return jnp.concatenate(rows, axis=0)
+
+
+def greet(peers):
+    barrier = pltpu.get_barrier_semaphore()
+    for peer in peers:
+        pl.semaphore_signal(barrier, inc=1, device_id=peer, device_id_type=MESH)
+    pl.semaphore_wait(barrier, len(peers))
+
+
+def forward_kernel(
+    n, group, steps, share,
+    feat, left, right, weight, table, obs, lat, out,
+    wpad, band, proj, dec, flat, recv, send, cot, ssem1, rsem1, ssem2, rsem2,
+):
     s = pl.program_id(0)
+    me = lax.axis_index("ens")
+    real = group * 2 * O
+    own = pl.multiple_of(me * share, 16)
+
+    def first(q, off):
+        peer = lax.rem(me + off, n)
+        return pltpu.make_async_remote_copy(
+            src_ref=dec.at[q, pl.ds(pl.multiple_of(peer * share, 16), share)],
+            dst_ref=recv.at[q, off],
+            send_sem=ssem1.at[q, off],
+            recv_sem=rsem1.at[q, off],
+            device_id={"ens": peer},
+            device_id_type=MESH,
+        )
+
+    def second(q, off):
+        return pltpu.make_async_remote_copy(
+            src_ref=send.at[q, off],
+            dst_ref=cot.at[q, pl.ds(own, share)],
+            send_sem=ssem2.at[q, off],
+            recv_sem=rsem2.at[q, off],
+            device_id={"ens": lax.rem(me - off + n, n)},
+            device_id_type=MESH,
+        )
 
     def put(values, h, lo):
         for k in range(K):
@@ -61,14 +116,21 @@
 
     @pl.when(s == 0)
     def _():
-        put(jnp.dot(weight[...], left[...], preferred_element_type=F32), 0, 0)
+        greet([{"ens": lax.rem(me + off, n)} for off in range(1, n)])
+        wpad[...] = padded_weight(weight).astype(BF16)
+        build_band(table, band)
+        if n * share > real:
+            for q in range(steps):
+                dec[q, real:, :] = jnp.zeros((n * share - real, HALF), BF16)
+            flat[real:, :] = jnp.zeros((n * share - real, HALF), F32)
+        put(jnp.dot(wpad[...], left[...], preferred_element_type=F32), 0, 0)
 
     @pl.when(s < steps)
     def _():
-        def one(n, carry):
-            lanes = pl.ds(pl.multiple_of(n * BLK, BLK), BLK)
-            got = jnp.dot(weight[...], feat[:, lanes], preferred_element_type=F32)
-            h = s * group + n
+        def one(b, carry):
+            lanes = pl.ds(pl.multiple_of(b * BLK, BLK), BLK)
+            got = jnp.dot(wpad[...], feat[:, lanes], preferred_element_type=F32)
+            h = s * group + b
             put(got[:, :HALF], h, HALF)
             put(got[:, HALF:], h + 1, 0)
             return carry
@@ -77,11 +139,12 @@
 
     @pl.when(s == steps)
     def _():
-        put(jnp.dot(weight[...], right[...], preferred_element_type=F32), steps * group, HALF)
-
-    @pl.when(s > 0)
-    def _():
-        g0 = (s - 1) * group
+        put(jnp.dot(wpad[...], right[...], preferred_element_type=F32), steps * group, HALF)
+
+    @pl.when(jnp.logical_and(s > 0, s <= steps))
+    def _():
+        q = s - 1
+        g0 = q * group
         acc = jnp.zeros((group * OP, BLK), F32)
         for k in range(K):
             for part in range(2):
@@ -92,121 +155,95 @@
         for g in range(group):
             piece = acc[g * OP : g * OP + O]
             both = jnp.concatenate([piece[:, :HALF], piece[:, HALF:]], axis=0)
-            out[g * 2 * O : (g + 1) * 2 * O, :] = both.astype(BF16)
-
-
-def forward(feat, left, right, weight, band, group, steps, rows):
+            dec[q, g * 2 * O : (g + 1) * 2 * O, :] = both.astype(BF16)
+        for off in range(1, n):
+            first(q, off).start()
+
+    @pl.when(s > 1)
+    def _():
+        q = s - 2
+        for t in range(2 * group):
+            flat[t * O : (t + 1) * O, :] = obs[:, t * HALF : (t + 1) * HALF]
+        for off in range(1, n):
+            first(q, off).wait_recv()
+        lat_row = jnp.broadcast_to(lat[0:1, :], (16, HALF))
+
+        def smooth(diff):
+            return diff * lax.rsqrt(diff * diff + SMOOTH * SMOOTH)
+
+        def one(step, carry):
+            at = pl.multiple_of(step * 16, 16)
+            here = pl.ds(pl.multiple_of(own + at, 16), 16)
+            values = [dec[q, here, :].astype(F32)]
+            values += [recv[q, off, pl.ds(at, 16), :].astype(F32) for off in range(1, n)]
+            sums = [None] * n
+            for a in range(n):
+                for b in range(a + 1, n):
+                    pair = smooth(values[a] - values[b])
+                    sums[a] = pair if sums[a] is None else sums[a] + pair
+                    sums[b] = -pair if sums[b] is None else sums[b] - pair
+            target = flat[here, :]
+            for a in range(n):
+                slope = smooth(values[a] - target) - sums[a] * (1.0 / (n - 1))
+                result = (slope * lat_row).astype(BF16)
+                if a == 0:
+                    cot[q, here, :] = result
+                else:
+                    send[q, a, pl.ds(at, 16), :] = result
+            return carry
+
+        lax.fori_loop(0, share // 16, one, 0)
+        for off in range(1, n):
+            second(q, off).start()
+
+    @pl.when(s == steps + 1)
+    def _():
+        for q in range(steps):
+            for off in range(1, n):
+                first(q, off).wait_send()
+                second(q, off).wait()
+        for q in range(steps):
+            out[q * n * share : (q + 1) * n * share, :] = cot[q]
+
+
+def forward(n, feat, left, right, weight, table, obs, lat, group, steps, share):
     chan = feat.shape[0]
     wide = group * BLK
+    rows = n * share
+    sem = pltpu.SemaphoreType.DMA((steps, n))
     return pl.pallas_call(
-        functools.partial(forward_kernel, group, steps),
-        out_shape=jax.ShapeDtypeStruct((rows, HALF), BF16),
-        grid=(steps + 1,),
+        functools.partial(forward_kernel, n, group, steps, share),
+        out_shape=jax.ShapeDtypeStruct((steps * rows, HALF), BF16),
+        grid=(steps + 2,),
         in_specs=[
             pl.BlockSpec((chan, wide), lambda s: (0, jnp.minimum(s, steps - 1))),
             whole(left.shape),
             whole(right.shape),
             whole(weight.shape),
-            whole(band.shape),
+            whole(table.shape),
+            pl.BlockSpec((O, wide), lambda s: (0, jnp.clip(s - 2, 0, steps - 1))),
+            whole(lat.shape),
         ],
-        out_specs=pl.BlockSpec((group * 2 * O, HALF), lambda s: (jnp.maximum(s - 1, 0), 0)),
-        scratch_shapes=[pltpu.VMEM((K, steps * group + 1, OP, BLK), BF16)],
-        compiler_params=pltpu.CompilerParams(vmem_limit_bytes=VMEM_LIMIT),
-        name="forward_conv",
-    )(feat, left, right, weight, band)
-
-
-def greet(peers):
-    barrier = pltpu.get_barrier_semaphore()
-    for peer in peers:
-        pl.semaphore_signal(barrier, inc=1, device_id=peer, device_id_type=MESH)
-    pl.semaphore_wait(barrier, len(peers))
-
-
-def slope_kernel(n, dec, obs, lat, cot, recv, send, ssem1, rsem1, ssem2, rsem2):
-    me = lax.axis_index("ens")
-    rows = obs.shape[0]
-    greet([{"ens": lax.rem(me + off, n)} for off in range(1, n)])
-    first = []
-    for off in range(1, n):
-        peer = lax.rem(me + off, n)
-        copy = pltpu.make_async_remote_copy(
-            src_ref=dec.at[pl.ds(pl.multiple_of(peer * rows, 16), rows)],
-            dst_ref=recv.at[off],
-            send_sem=ssem1.at[off],
-            recv_sem=rsem1.at[off],
-            device_id={"ens": peer},
-            device_id_type=MESH,
-        )
-        copy.start()
-        first.append(copy)
-    for copy in first:
-        copy.wait()
-    own = pl.multiple_of(me * rows, 16)
-    lat_row = jnp.broadcast_to(lat[0:1, :], (16, HALF))
-
-    def smooth(diff):
-        return diff * lax.rsqrt(diff * diff + SMOOTH * SMOOTH)
-
-    def one(step, carry):
-        at = pl.multiple_of(step * 16, 16)
-        values = [dec[pl.ds(pl.multiple_of(own + at, 16), 16), :].astype(F32)]
-        values += [recv[off, pl.ds(at, 16), :].astype(F32) for off in range(1, n)]
-        sums = [None] * n
-        for a in range(n):
-            for b in range(a + 1, n):
-                pair = smooth(values[a] - values[b])
-                sums[a] = pair if sums[a] is None else sums[a] + pair
-                sums[b] = -pair if sums[b] is None else sums[b] - pair
-        target = obs[pl.ds(at, 16), :]
-        for a in range(n):
-            slope = smooth(values[a] - target) - sums[a] * (1.0 / (n - 1))
-            result = (slope * lat_row).astype(BF16)
-            if a == 0:
-                cot[pl.ds(pl.multiple_of(own + at, 16), 16), :] = result
-            else:
-                send[a, pl.ds(at, 16), :] = result
-        return carry
-
-    lax.fori_loop(0, rows // 16, one, 0)
-    second = []
-    for off in range(1, n):
-        peer = lax.rem(me - off + n, n)
-        copy = pltpu.make_async_remote_copy(
-            src_ref=send.at[off],
-            dst_ref=cot.at[pl.ds(own, rows)],
-            send_sem=ssem2.at[off],
-            recv_sem=rsem2.at[off],
-            device_id={"ens": peer},
-            device_id_type=MESH,
-        )
-        copy.start()
-        second.append(copy)
-    for copy in second:
-        copy.wait()
-
-
-def slopes(n, dec, obs, lat):
-    rows = obs.shape[0]
-    vmem = pl.BlockSpec(memory_space=pltpu.VMEM)
-    return pl.pallas_call(
-        functools.partial(slope_kernel, n),
-        out_shape=jax.ShapeDtypeStruct(dec.shape, BF16),
-        in_specs=[vmem] * 3,
-        out_specs=vmem,
+        out_specs=whole((steps * rows, HALF)),
         scratch_shapes=[
-            pltpu.VMEM((n, rows, HALF), BF16),
-            pltpu.VMEM((n, rows, HALF), BF16),
-            pltpu.SemaphoreType.DMA((n,)),
-            pltpu.SemaphoreType.DMA((n,)),
-            pltpu.SemaphoreType.DMA((n,)),
-            pltpu.SemaphoreType.DMA((n,)),
+            pltpu.VMEM((K * OP, chan), BF16),
+            pltpu.VMEM((K, 2 * BLK, BLK), BF16),
+            pltpu.VMEM((K, steps * group + 1, OP, BLK), BF16),
+            pltpu.VMEM((steps, rows, HALF), BF16),
+            pltpu.VMEM((rows, HALF), F32),
+            pltpu.VMEM((steps, n, share, HALF), BF16),
+            pltpu.VMEM((steps, n, share, HALF), BF16),
+            pltpu.VMEM((steps, rows, HALF), BF16),
+            sem,
+            sem,
+            sem,
+            sem,
         ],
         compiler_params=pltpu.CompilerParams(
             collective_id=0, has_side_effects=True, vmem_limit_bytes=VMEM_LIMIT
         ),
-        name="member_slopes",
-    )(dec, obs, lat)
+        name="forward_slopes",
+    )(feat, left, right, weight, table, obs, lat)
 
 
 WG_ROWS = 2048
@@ -214,7 +251,9 @@
 
 
 def backward_kernel(
-    group, steps, cells, padded, cot, left, right, weight_t, band, feat, grad, wgrad, ext, spread, acc
+    group, steps, share, cells, padded,
+    cot, left, right, weight, table, feat, grad, wgrad,
+    weight_t, band, ext, spread, acc,
 ):
     s = pl.program_id(0)
     blocks = steps * group
@@ -225,8 +264,12 @@
         ext[0, :O, :HALF] = left[...]
         ext[blocks, :O, HALF:] = right[...]
 
+        weight_t[...] = padded_weight(weight).T.astype(BF16)
+        build_band(table, band)
+
         def one(b, carry):
-            pair = cot[pl.ds(pl.multiple_of(b * 2 * O, 16), 2 * O), :].astype(F32)
+            start = lax.div(b, group) * share + lax.rem(b, group) * (2 * O)
+            pair = cot[pl.ds(pl.multiple_of(start, 16), 2 * O), :].astype(F32)
             ext[b, :O, HALF:] = pair[:O].astype(BF16)
             ext[b + 1, :O, :HALF] = pair[O:].astype(BF16)
             return carry
@@ -274,12 +317,14 @@
             wgrad[t * WG_PART : (t + 1) * WG_PART, :] = jnp.concatenate(rows, axis=0).astype(BF16)
 
 
-def backward(cot, left, right, weight_t, band, feat, group, steps, cells):
+def backward(cot, left, right, weight, table, feat, group, steps, cells):
     chan = feat.shape[0]
     wide = group * BLK
     blocks = steps * group
     return pl.pallas_call(
-        functools.partial(backward_kernel, group, steps, cells, cells != blocks * BLK),
+        functools.partial(
+            backward_kernel, group, steps, cot.shape[0] // steps, cells, cells != blocks * BLK
+        ),
         out_shape=(
             jax.ShapeDtypeStruct(feat.shape, BF16),
             jax.ShapeDtypeStruct((WG_ROWS, HALF), BF16),
@@ -289,19 +334,21 @@
             whole(cot.shape),
             whole(left.shape),
             whole(right.shape),
-            whole(weight_t.shape),
-            whole(band.shape),
+            whole(weight.shape),
+            whole(table.shape),
             pl.BlockSpec((chan, wide), lambda s: (0, s)),
         ],
         out_specs=(pl.BlockSpec((chan, wide), lambda s: (0, s)), whole((WG_ROWS, HALF))),
         scratch_shapes=[
+            pltpu.VMEM((chan, K * OP), BF16),
+            pltpu.VMEM((K, 2 * BLK, BLK), BF16),
             pltpu.VMEM((blocks + 1, OP, BLK), BF16),
             pltpu.VMEM((K * OP, wide), BF16),
             pltpu.VMEM((K * OP, chan), F32),
         ],
         compiler_params=pltpu.CompilerParams(vmem_limit_bytes=VMEM_LIMIT),
         name="backward_conv",
-    )(cot, left, right, weight_t, band, feat)
+    )(cot, left, right, weight, table, feat)
 
 
 def reduce_kernel(ne, nl, scale, part, out, recv1, mid, recv2, got, *sems):
@@ -435,43 +482,39 @@
     blocks = cells // BLK if aligned else pl.cdiv(cells + HALF, BLK)
     group = max(g for g in range(1, 10) if blocks % g == 0)
     steps = blocks // group
-    tiles = 2 * blocks
-    per = pl.cdiv(tiles, ne)
-    per += per % 2
-    rows = per * ne * O
+    real = group * 2 * O
+    share = pl.cdiv(pl.cdiv(real, ne), 16) * 16
+    rows = ne * share
     extra = blocks * BLK - cells
 
     left = passed_along(feat[:, cells - HALF :], "lon", 1)
     right = passed_along(feat[:, :HALF], "lon", -1)
-    ahead, back = band_tables(kernel_rows(basis_vals, row_of, col_off))
-    weight = jnp.pad(proj_weight.reshape(K, O, chan), ((0, 0), (0, OP - O), (0, 0)))
-    weight = weight.reshape(K * OP, chan)
+    ahead, back = side_tables(kernel_rows(basis_vals, row_of, col_off))
     if not aligned:
         feat = jnp.pad(jnp.concatenate([feat, right], axis=1), ((0, 0), (0, extra - HALF)))
         right = jnp.zeros_like(right)
-    dec = forward(feat, left, right, weight, ahead, group, steps, rows)
-
-    obs = jnp.pad(observed, ((0, 0), (0, per * ne * HALF - cells)))
-    obs = lax.dynamic_slice_in_dim(obs, lax.axis_index("ens") * per * HALF, per * HALF, axis=1)
-    obs = obs.reshape(O, per, HALF).transpose(1, 0, 2).reshape(per * O, HALF)
+        observed = jnp.pad(observed, ((0, 0), (0, extra)))
     lat = jnp.broadcast_to(jnp.tile(lat_weight, HALF // LAT)[None, :], (8, HALF))
-    cot = slopes(ne, dec, obs, lat)
+    cot = forward(
+        ne, feat, left, right, proj_weight, ahead, observed, lat, group, steps, share
+    )
 
     if aligned:
-        cot_left = passed_along(cot[(tiles - 1) * O : tiles * O], "lon", 1)
+        last = (steps - 1) * rows + real
+        cot_left = passed_along(cot[last - O : last], "lon", 1)
         cot_right = passed_along(cot[:O], "lon", -1)
     else:
-        flat = cot.reshape(per * ne, O, HALF).transpose(1, 0, 2).reshape(O, per * ne * HALF)
-        flat = flat[:, :cells]
+        flat = cot.reshape(steps, rows, HALF)[:, :real].reshape(2 * blocks, O, HALF)
+        flat = flat.transpose(1, 0, 2).reshape(O, blocks * BLK)[:, :cells]
         cot_left = passed_along(flat[:, cells - HALF :], "lon", 1)
         cot_right = passed_along(flat[:, :HALF], "lon", -1)
         flat = jnp.pad(
-            jnp.concatenate([flat, cot_right], axis=1),
-            ((0, 0), (0, per * ne * HALF - cells - HALF)),
+            jnp.concatenate([flat, cot_right], axis=1), ((0, 0), (0, extra - HALF))
         )
-        cot = flat.reshape(O, per * ne, HALF).transpose(1, 0, 2).reshape(rows, HALF)
+        flat = flat.reshape(O, 2 * blocks, HALF).transpose(1, 0, 2).reshape(steps, real, HALF)
+        cot = jnp.pad(flat, ((0, 0), (0, rows - real), (0, 0))).reshape(steps * rows, HALF)
         cot_right = jnp.zeros_like(cot_right)
-    grad, part = backward(cot, cot_left, cot_right, weight.T, back, feat, group, steps, cells)
+    grad, part = backward(cot, cot_left, cot_right, proj_weight, back, feat, group, steps, cells)
     scale = 1.0 / math.sqrt(ne * (cells // LAT) * nl * LAT)
     weight_grad = reduced(ne, nl, scale, part, chan)
     return (grad[:, :cells][None], weight_grad)

time: 206 us -> 152 us (0.74)
  local copies, waits for them, and re-layouts: 48.3 us -> 8.27 us
  Pallas kernels: 147 us -> 131 us
  waiting for transfers between devices: 0.01 us -> 4.37 us
    concatenate x2 -> x0, local copies, waits for them, and re-layouts: 19.8 us -> none  [band_tables(): out.append(jnp.concatenate(parts, axis=2))]
    pallas_call x3 -> x2, Pallas kernels: 118 us -> 102 us  [the longest x1 61.4 us: forward(): pl.pallas_call(functools.partial(forward_kernel, n, group, steps, share),...]
    pad x3 -> x0, local copies, waits for them, and re-layouts: 11.6 us -> none  [the longest x2 10.8 us: band_tables(): jnp.pad(base, ((0, 0), (j, 2 * cols - taps - j), (0, 0), (0, 0)))]
    ppermute x4, waiting for transfers between devices: 0.01 us -> 4.37 us  [passed_along(): lax.ppermute(value, axis, [(i, (i + steps) % count) for i in range(count)])]
    reshape x2 -> x0, local copies, waits for them, and re-layouts: 2.99 us -> none  [the longest x1 1.92 us: shards(): obs = obs.reshape(O, per, HALF).transpose(1, 0, 2).reshape(per * O, HALF)]
    unnamed x18 -> x13, local copies, waits for them, and re-layouts: 5.75 us -> 2.86 us
  transfers between devices with their start and end apart: 4 -> 4, of which waited for: 0 -> 2; matrix products, arithmetic and copies ran while one was open for 21% -> 3% of each run, Pallas kernels for 0% -> 0%
where the time goes in v2:
time: 152 us; the launch traced here: 151 us
  Pallas kernels  131 us (86%)
  local copies, waits for them, and re-layouts  8.27 us (5%)
  starting transfers between devices  5.66 us (4%)
  waiting for transfers between devices  4.37 us (3%)
    pallas_call x1, Pallas kernels, forward(): pl.pallas_call(functools.partial(forward_kernel, n, group, steps, share),...  61.4 us
    pallas_call x1, Pallas kernels, backward(): pl.pallas_call(functools.partial(backward_kernel, group, steps, cot.shape...  40.6 us
    pallas_call x1, Pallas kernels, reduced(): pl.pallas_call(body, out_shape=jax.ShapeDtypeStruct((K * O, chan), F32),...  28.9 us
    ppermute x4, starting transfers between devices, passed_along(): lax.ppermute(value, axis, [(i, (i + steps) % count) for i in range(count)])  5.66 us
    ppermute x4, waiting for transfers between devices, passed_along(): lax.ppermute(value, axis, [(i, (i + steps) % count) for i in range(count)])  4.37 us
  transfers between devices with their start and end apart: 4, of which 2 were waited for; matrix products, arithmetic and copies ran while one was open for 3% of the time, Pallas kernels for 0%

profile of v2, /device:TPU:1, one launch (start us, length us, event | category | flops | bytes accessed | tf_op | source)
XLA Modules:
  0.0 151.4 jit_solution(17540381846979573202)
XLA Ops:
  0.6 0.0 copy-start
  0.6 1.0 fusion.5
  1.6 4.2 %collective-permute-start.1 = (bf16[384,128]{1,0:T(8,128)(2,1)S(1)}, bf16[384,128]{1,0:T(8,128)(2,1)S(1)}, u32[]{:S(2)}, u32[]{:S(2)}) collective-permute-start(bf16[384,128]{1,0:T(8,128)(2,1)S(1)} %get-tuple-element.6), channel_id=1, source_target_pairs={{0,3},{1,0},{2,1},{3,2},{4,7},{5,4},{6,5},{7,6},{8,11},{9,8},{10,9... | collective-permute-start | bytes 294920 | tf_op jit(solution)/shard_map/ppermute | solution.py:472
  5.8 0.0 collective-permute-start
  5.8 0.7 multiply_add_fusion
  6.6 0.0 copy-done
  6.6 0.8 fusion.2
  7.4 0.7 tile.2
  8.0 0.1 broadcast_in_dim.12
  8.1 1.2 copy.13
  9.3 0.0 collective-permute-done.1.right
  9.3 1.8 %collective-permute-done.left = bf16[384,128]{1,0:T(8,128)(2,1)S(1)} collective-permute-done((bf16[384,128]{1,0:T(8,128)(2,1)S(1)}, bf16[384,128]{1,0:T(8,128)(2,1)S(1)}, u32[]{:S(2)}, u32[]{:S(2)}) %collective-permute-start) | collective-permute-done | bytes 98336 | tf_op jit(solution)/shard_map/ppermute | solution.py:472
  11.1 0.0 copy-start.3
  11.1 0.6 broadcast_in_dim.13.lat
  11.7 0.0 copy-done.2
  11.7 0.0 copy-done.3
  11.7 0.0 copy-start.1
  11.7 61.4 %forward_slopes.1.cot = bf16[7040,128]{1,0:T(8,128)(2,1)} custom-call(bf16[384,11520]{1,0:T(8,128)(2,1)} %bitcast.13, bf16[384,128]{1,0:T(8,128)(2,1)} %copy-done.3, bf16[384,128]{1,0:T(8,128)(2,1)} %copy-done.2, bf16[648,384]{1,0:T(8,128)(2,1)} %weight.3, bf16[9,288,32]{2,1,0:T(8,128)(2,1)} %bitcast.15, f32[72,11520]{1,0:T(8,128)} %obs.1, ...), custom_call_target="tpu_custom_call" | custom-call | tf_op jit(solution)/shard_map/forward_slopes/pallas_call | solution.py:214
  73.2 0.7 fusion.6
  73.9 0.8 collective-permute-start.3
  74.7 0.7 collective-permute-start.2
  75.4 0.0 copy-done.1
  75.5 1.1 copy.14
  76.6 0.0 collective-permute-done.3.right
  76.6 0.0 copy-start.4
  76.6 2.5 %collective-permute-done.2.left = bf16[72,128]{1,0:T(8,128)(2,1)S(1)} collective-permute-done((bf16[72,128]{1,0:T(8,128)(2,1)S(1)}, bf16[72,128]{1,0:T(8,128)(2,1)S(1)}, u32[]{:S(2)}, u32[]{:S(2)}) %collective-permute-start.2) | collective-permute-done | bytes 18464 | tf_op jit(solution)/shard_map/ppermute | solution.py:472
  79.1 0.0 copy-start.5
  79.1 0.0 copy-done.4
  79.1 0.6 copy-done.5
  79.7 40.6 %backward_conv.1 = (bf16[384,11520]{1,0:T(8,128)(2,1)}, bf16[2048,128]{1,0:T(8,128)(2,1)}) custom-call(bf16[7040,128]{1,0:T(8,128)(2,1)} %forward_slopes.1.cot, bf16[72,128]{1,0:T(8,128)(2,1)} %copy-done.5, bf16[72,128]{1,0:T(8,128)(2,1)} %copy-done.4, bf16[648,384]{1,0:T(8,128)(2,1)} %weight.3, bf16[9,288,32]{2,1,0:T(8,128)(2,1)} %bitcast.17, ...), custom_call_target="tpu_custom_call" | custom-call | tf_op jit(solution)/shard_map/backward_conv/pallas_call | solution.py:324
  120.3 28.9 %weight_reduce.1 = f32[648,384]{1,0:T(8,128)} custom-call(bf16[2048,128]{1,0:T(8,128)(2,1)} %get-tuple-element.5.part), custom_call_target="tpu_custom_call" | custom-call | tf_op jit(solution)/shard_map/weight_reduce/pallas_call | solution.py:450
  149.2 2.2 %copy.18 = f32[648,384]{1,0:T(8,128)} copy(f32[648,384]{1,0:T(8,128)} %weight_reduce.1) | data formatting | bytes 1990656
  (2 shorter events, 0.0 us)
Async XLA Ops:
  0.6 6.0 %copy-start = (f32[32,32,9]{1,0,2:T(8,128)S(1)}, f32[32,32,9]{1,0,2:T(8,128)}, u32[]{:S(2)}) copy-start(f32[32,32,9]{1,0,2:T(8,128)} %param.9) | copy-start | bytes 110596
  1.6 7.6 %collective-permute-start.1 = (bf16[384,128]{1,0:T(8,128)(2,1)S(1)}, bf16[384,128]{1,0:T(8,128)(2,1)S(1)}, u32[]{:S(2)}, u32[]{:S(2)}) collective-permute-start(bf16[384,128]{1,0:T(8,128)(2,1)S(1)} %get-tuple-element.6), channel_id=1, source_target_pairs={{0,3},{1,0},{2,1},{3,2},{4,7},{5,4},{6,5},{7,6},{8,11},{9,8},{10,9... | collective-permute-start | bytes 294920 | tf_op jit(solution)/shard_map/ppermute | solution.py:472
  5.8 5.3 %collective-permute-start = (bf16[384,128]{1,0:T(8,128)(2,1)S(1)}, bf16[384,128]{1,0:T(8,128)(2,1)S(1)}, u32[]{:S(2)}, u32[]{:S(2)}) collective-permute-start(bf16[384,128]{1,0:T(8,128)(2,1)S(1)} %get-tuple-element.7), channel_id=1, source_target_pairs={{0,1},{1,2},{2,3},{3,0},{4,5},{5,6},{6,7},{7,4},{8,9},{9,10},{10,1... | collective-permute-start | bytes 294920 | tf_op jit(solution)/shard_map/ppermute | solution.py:472
  9.3 2.5 %copy-start.2 = (bf16[384,128]{1,0:T(8,128)(2,1)}, bf16[384,128]{1,0:T(8,128)(2,1)S(1)}, u32[]{:S(2)}) copy-start(bf16[384,128]{1,0:T(8,128)(2,1)S(1)} %collective-permute-done.1.right) | copy-start | bytes 294916
  11.1 0.6 copy-start.3
  11.7 63.7 %copy-start.1 = (bf16[32,9,288]{0,2,1:T(8,128)(2,1)S(1)}, bf16[32,9,288]{0,2,1:T(8,128)(2,1)}, u32[]{:S(2)}) copy-start(bf16[32,9,288]{0,2,1:T(8,128)(2,1)} %copy.13) | copy-start | bytes 497668
  73.9 2.6 %collective-permute-start.3 = (bf16[72,128]{1,0:T(8,128)(2,1)S(1)}, bf16[72,128]{1,0:T(8,128)(2,1)S(1)}, u32[]{:S(2)}, u32[]{:S(2)}) collective-permute-start(bf16[72,128]{1,0:T(8,128)(2,1)S(1)} %get-tuple-element.8), channel_id=1, source_target_pairs={{0,3},{1,0},{2,1},{3,2},{4,7},{5,4},{6,5},{7,6},{8,11},{9,8},{10,9... | collective-permute-start | bytes 55304 | tf_op jit(solution)/shard_map/ppermute | solution.py:472
  74.7 4.4 %collective-permute-start.2 = (bf16[72,128]{1,0:T(8,128)(2,1)S(1)}, bf16[72,128]{1,0:T(8,128)(2,1)S(1)}, u32[]{:S(2)}, u32[]{:S(2)}) collective-permute-start(bf16[72,128]{1,0:T(8,128)(2,1)S(1)} %get-tuple-element.9), channel_id=1, source_target_pairs={{0,1},{1,2},{2,3},{3,0},{4,5},{5,6},{6,7},{7,4},{8,9},{9,10},{10,1... | collective-permute-start | bytes 55304 | tf_op jit(solution)/shard_map/ppermute | solution.py:472
  76.6 2.6 %copy-start.4 = (bf16[72,128]{1,0:T(8,128)(2,1)}, bf16[72,128]{1,0:T(8,128)(2,1)S(1)}, u32[]{:S(2)}) copy-start(bf16[72,128]{1,0:T(8,128)(2,1)S(1)} %collective-permute-done.3.right) | copy-start | bytes 55300
  79.1 0.6 copy-start.5

commit v3 on v2

--- a/solution.py
+++ b/solution.py
@@ -80,14 +80,27 @@
 
 
 def forward_kernel(
-    n, group, steps, share,
-    feat, left, right, weight, table, obs, lat, out,
-    wpad, band, proj, dec, flat, recv, send, cot, ssem1, rsem1, ssem2, rsem2,
+    n, nl, group, steps, share,
+    feat, tail, head, weight, table, obs, lat, out, rims,
+    wpad, band, proj, dec, flat, recv, send, cot, left, right, rim_left, rim_right,
+    ssem1, rsem1, ssem2, rsem2, hsend, hrecv,
 ):
     s = pl.program_id(0)
     me = lax.axis_index("ens")
     real = group * 2 * O
     own = pl.multiple_of(me * share, 16)
+    after = {"lon": lax.rem(lax.axis_index("lon") + 1, nl)}
+    before = {"lon": lax.rem(lax.axis_index("lon") + nl - 1, nl)}
+
+    def rim(src, dst, slot, peer):
+        return pltpu.make_async_remote_copy(
+            src_ref=src,
+            dst_ref=dst,
+            send_sem=hsend.at[slot],
+            recv_sem=hrecv.at[slot],
+            device_id=peer,
+            device_id_type=MESH,
+        )
 
     def first(q, off):
         peer = lax.rem(me + off, n)
@@ -116,14 +129,15 @@
 
     @pl.when(s == 0)
     def _():
-        greet([{"ens": lax.rem(me + off, n)} for off in range(1, n)])
+        greet([{"ens": lax.rem(me + off, n)} for off in range(1, n)] + [after, before])
+        rim(tail, left, 0, after).start()
+        rim(head, right, 1, before).start()
         wpad[...] = padded_weight(weight).astype(BF16)
         build_band(table, band)
         if n * share > real:
             for q in range(steps):
                 dec[q, real:, :] = jnp.zeros((n * share - real, HALF), BF16)
             flat[real:, :] = jnp.zeros((n * share - real, HALF), F32)
-        put(jnp.dot(wpad[...], left[...], preferred_element_type=F32), 0, 0)
 
     @pl.when(s < steps)
     def _():
@@ -137,8 +151,14 @@
 
         lax.fori_loop(0, group, one, 0)
 
+    @pl.when(s == 1)
+    def _():
+        rim(tail, left, 0, after).wait()
+        put(jnp.dot(wpad[...], left[...], preferred_element_type=F32), 0, 0)
+
     @pl.when(s == steps)
     def _():
+        rim(head, right, 1, before).wait()
         put(jnp.dot(wpad[...], right[...], preferred_element_type=F32), steps * group, HALF)
 
     @pl.when(jnp.logical_and(s > 0, s <= steps))
@@ -202,29 +222,40 @@
             for off in range(1, n):
                 first(q, off).wait_send()
                 second(q, off).wait()
+        last = rim(cot.at[steps - 1, pl.ds(real - OP, OP)], rim_left, 2, after)
+        opening = rim(cot.at[0, pl.ds(0, OP)], rim_right, 3, before)
+        last.start()
+        opening.start()
         for q in range(steps):
             out[q * n * share : (q + 1) * n * share, :] = cot[q]
-
-
-def forward(n, feat, left, right, weight, table, obs, lat, group, steps, share):
+        last.wait()
+        opening.wait()
+        rims[0] = rim_left[...]
+        rims[1] = rim_right[...]
+
+
+def forward(n, nl, feat, tail, head, weight, table, obs, lat, group, steps, share):
     chan = feat.shape[0]
     wide = group * BLK
     rows = n * share
     sem = pltpu.SemaphoreType.DMA((steps, n))
     return pl.pallas_call(
-        functools.partial(forward_kernel, n, group, steps, share),
-        out_shape=jax.ShapeDtypeStruct((steps * rows, HALF), BF16),
+        functools.partial(forward_kernel, n, nl, group, steps, share),
+        out_shape=(
+            jax.ShapeDtypeStruct((steps * rows, HALF), BF16),
+            jax.ShapeDtypeStruct((2, OP, HALF), BF16),
+        ),
         grid=(steps + 2,),
         in_specs=[
             pl.BlockSpec((chan, wide), lambda s: (0, jnp.minimum(s, steps - 1))),
-            whole(left.shape),
-            whole(right.shape),
+            whole(tail.shape),
+            whole(head.shape),
             whole(weight.shape),
             whole(table.shape),
             pl.BlockSpec((O, wide), lambda s: (0, jnp.clip(s - 2, 0, steps - 1))),
             whole(lat.shape),
         ],
-        out_specs=whole((steps * rows, HALF)),
+        out_specs=(whole((steps * rows, HALF)), whole((2, OP, HALF))),
         scratch_shapes=[
             pltpu.VMEM((K * OP, chan), BF16),
             pltpu.VMEM((K, 2 * BLK, BLK), BF16),
@@ -234,16 +265,22 @@
             pltpu.VMEM((steps, n, share, HALF), BF16),
             pltpu.VMEM((steps, n, share, HALF), BF16),
             pltpu.VMEM((steps, rows, HALF), BF16),
+            pltpu.VMEM((chan, HALF), BF16),
+            pltpu.VMEM((chan, HALF), BF16),
+            pltpu.VMEM((OP, HALF), BF16),
+            pltpu.VMEM((OP, HALF), BF16),
             sem,
             sem,
             sem,
             sem,
+            pltpu.SemaphoreType.DMA((4,)),
+            pltpu.SemaphoreType.DMA((4,)),
         ],
         compiler_params=pltpu.CompilerParams(
             collective_id=0, has_side_effects=True, vmem_limit_bytes=VMEM_LIMIT
         ),
         name="forward_slopes",
-    )(feat, left, right, weight, table, obs, lat)
+    )(feat, tail, head, weight, table, obs, lat)
 
 
 WG_ROWS = 2048
@@ -251,7 +288,7 @@
 
 
 def backward_kernel(
-    group, steps, share, cells, padded,
+    group, steps, piece, share, cells, padded,
     cot, left, right, weight, table, feat, grad, wgrad,
     weight_t, band, ext, spread, acc,
 ):
@@ -261,14 +298,14 @@
     @pl.when(s == 0)
     def _():
         ext[:, O:, :] = jnp.zeros((blocks + 1, OP - O, BLK), BF16)
-        ext[0, :O, :HALF] = left[...]
-        ext[blocks, :O, HALF:] = right[...]
+        ext[0, :O, :HALF] = left[...].astype(F32)[OP - O :].astype(BF16)
+        ext[blocks, :O, HALF:] = right[:O]
 
         weight_t[...] = padded_weight(weight).T.astype(BF16)
         build_band(table, band)
 
         def one(b, carry):
-            start = lax.div(b, group) * share + lax.rem(b, group) * (2 * O)
+            start = lax.div(b, piece) * share + lax.rem(b, piece) * (2 * O)
             pair = cot[pl.ds(pl.multiple_of(start, 16), 2 * O), :].astype(F32)
             ext[b, :O, HALF:] = pair[:O].astype(BF16)
             ext[b + 1, :O, :HALF] = pair[O:].astype(BF16)
@@ -317,13 +354,19 @@
             wgrad[t * WG_PART : (t + 1) * WG_PART, :] = jnp.concatenate(rows, axis=0).astype(BF16)
 
 
-def backward(cot, left, right, weight, table, feat, group, steps, cells):
+def backward(cot, left, right, weight, table, feat, group, steps, piece, cells):
     chan = feat.shape[0]
     wide = group * BLK
     blocks = steps * group
     return pl.pallas_call(
         functools.partial(
-            backward_kernel, group, steps, cot.shape[0] // steps, cells, cells != blocks * BLK
+            backward_kernel,
+            group,
+            steps,
+            piece,
+            cot.shape[0] * piece // blocks,
+            cells,
+            cells != blocks * BLK,
         ),
         out_shape=(
             jax.ShapeDtypeStruct(feat.shape, BF16),
@@ -480,29 +523,29 @@
     chan, cells = feat.shape
     aligned = cells % BLK == 0
     blocks = cells // BLK if aligned else pl.cdiv(cells + HALF, BLK)
-    group = max(g for g in range(1, 10) if blocks % g == 0)
+    group_back = max(g for g in range(1, 10) if blocks % g == 0)
+    steps_back = blocks // group_back
+    group = max(g for g in range(1, 7) if blocks % g == 0)
     steps = blocks // group
     real = group * 2 * O
     share = pl.cdiv(pl.cdiv(real, ne), 16) * 16
     rows = ne * share
     extra = blocks * BLK - cells
 
-    left = passed_along(feat[:, cells - HALF :], "lon", 1)
-    right = passed_along(feat[:, :HALF], "lon", -1)
+    tail = feat[:, cells - HALF :]
+    head = feat[:, :HALF]
     ahead, back = side_tables(kernel_rows(basis_vals, row_of, col_off))
     if not aligned:
+        right = passed_along(head, "lon", -1)
         feat = jnp.pad(jnp.concatenate([feat, right], axis=1), ((0, 0), (0, extra - HALF)))
-        right = jnp.zeros_like(right)
         observed = jnp.pad(observed, ((0, 0), (0, extra)))
     lat = jnp.broadcast_to(jnp.tile(lat_weight, HALF // LAT)[None, :], (8, HALF))
-    cot = forward(
-        ne, feat, left, right, proj_weight, ahead, observed, lat, group, steps, share
+    cot, rims = forward(
+        ne, nl, feat, tail, head, proj_weight, ahead, observed, lat, group, steps, share
     )
 
     if aligned:
-        last = (steps - 1) * rows + real
-        cot_left = passed_along(cot[last - O : last], "lon", 1)
-        cot_right = passed_along(cot[:O], "lon", -1)
+        cot_left, cot_right = rims[0], rims[1]
     else:
         flat = cot.reshape(steps, rows, HALF)[:, :real].reshape(2 * blocks, O, HALF)
         flat = flat.transpose(1, 0, 2).reshape(O, blocks * BLK)[:, :cells]
@@ -513,8 +556,11 @@
         )
         flat = flat.reshape(O, 2 * blocks, HALF).transpose(1, 0, 2).reshape(steps, real, HALF)
         cot = jnp.pad(flat, ((0, 0), (0, rows - real), (0, 0))).reshape(steps * rows, HALF)
-        cot_right = jnp.zeros_like(cot_right)
-    grad, part = backward(cot, cot_left, cot_right, proj_weight, back, feat, group, steps, cells)
+        cot_left = jnp.pad(cot_left, ((OP - O, 0), (0, 0)))
+        cot_right = jnp.zeros((OP, HALF), BF16)
+    grad, part = backward(
+        cot, cot_left, cot_right, proj_weight, back, feat, group_back, steps_back, group, cells
+    )
     scale = 1.0 / math.sqrt(ne * (cells // LAT) * nl * LAT)
     weight_grad = reduced(ne, nl, scale, part, chan)
     return (grad[:, :cells][None], weight_grad)

time: 152 us -> 142 us (0.934)
  starting transfers between devices: 5.66 us -> 0 us
  waiting for transfers between devices: 4.37 us -> 0 us
    ppermute x4 -> x0, starting transfers between devices: 5.66 us -> none  [passed_along(): lax.ppermute(value, axis, [(i, (i + steps) % count) for i in range(count)])]
    ppermute x4 -> x0, waiting for transfers between devices: 4.37 us -> none  [passed_along(): lax.ppermute(value, axis, [(i, (i + steps) % count) for i in range(count)])]
    pallas_call x2, Pallas kernels: 102 us -> 104 us  [the longest x1 63.3 us: forward(): pl.pallas_call(functools.partial(forward_kernel, n, nl, group, steps, sha...]
  transfers between devices with their start and end apart: 4 -> 0, of which waited for: 2 -> 0; matrix products, arithmetic and copies ran while one was open for 3% -> 0% of each run, Pallas kernels for 0% -> 0%
where the time goes in v3:
time: 142 us
  Pallas kernels  132 us (93%)
  local copies, waits for them, and re-layouts  8.14 us (6%)
    pallas_call x1, Pallas kernels, forward(): pl.pallas_call(functools.partial(forward_kernel, n, nl, group, steps, sha...  63.3 us
    pallas_call x1, Pallas kernels, backward(): pl.pallas_call(functools.partial(backward_kernel, group, steps, piece, co...  40.6 us
    pallas_call x1, Pallas kernels, reduced(): pl.pallas_call(body, out_shape=jax.ShapeDtypeStruct((K * O, chan), F32),...  27.9 us

profile of v3, /device:TPU:1, one launch (start us, length us, event | category | flops | bytes accessed | tf_op | source)
XLA Modules:
  0.0 142.1 jit_solution(4353596197731010589)
XLA Ops:
  0.6 0.0 copy-start
  0.6 0.7 tile.2
  1.3 0.1 broadcast_in_dim.12
  1.4 0.6 broadcast_in_dim.13.lat
  2.0 0.7 multiply_add_fusion
  2.8 1.6 %fusion.5 = (bf16[384,128]{1,0:T(8,128)(2,1)}, bf16[384,128]{1,0:T(8,128)(2,1)}) fusion(bf16[384,11520]{1,0:T(8,128)(2,1)} %bitcast.16), kind=kLoop, calls=%fused_computation.10 | loop fusion | bytes 393216 | tf_op jit(solution)/shard_map/slice | solution.py:536
  4.4 0.0 copy-done
  4.4 0.8 fusion.2
  5.2 0.4 copy.13
  5.6 0.0 copy-start.1
  5.6 1.1 copy.14
  6.7 0.0 copy-done.1
  6.7 63.3 %forward_slopes.1 = (bf16[6912,128]{1,0:T(8,128)(2,1)}, bf16[2,80,128]{2,1,0:T(8,128)(2,1)}) custom-call(bf16[384,11520]{1,0:T(8,128)(2,1)} %bitcast.17, bf16[384,128]{1,0:T(8,128)(2,1)} %get-tuple-element.11.tail, bf16[384,128]{1,0:T(8,128)(2,1)} %get-tuple-element.10.head, bf16[648,384]{1,0:T(8,128)(2,1)} %weight.3, bf16[9,288,32]{2,1,0:T(8,128)(2,1)} %bitcast.20, ...), custom_call_target="tpu_custom_call" | custom-call | tf_op jit(solution)/shard_map/forward_slopes/pallas_call | solution.py:242
  70.0 1.4 slice_bitcast_fusion
  71.4 40.6 %backward_conv.1 = (bf16[384,11520]{1,0:T(8,128)(2,1)}, bf16[2048,128]{1,0:T(8,128)(2,1)}) custom-call(bf16[6912,128]{1,0:T(8,128)(2,1)} %get-tuple-element.6.cot, bf16[80,128]{1,0:T(8,128)(2,1)} %get-tuple-element.13.left, bf16[80,128]{1,0:T(8,128)(2,1)} %get-tuple-element.12.right, bf16[648,384]{1,0:T(8,128)(2,1)} %weight.3, bf16[9,288,32]{2,1,0:T(8,128)(2,1)} %bitcast.21, ...), custom_call_target="tpu_custom_call" | custom-call | tf_op jit(solution)/shard_map/backward_conv/pallas_call | solution.py:361
  112.0 27.9 %weight_reduce.1 = f32[648,384]{1,0:T(8,128)} custom-call(bf16[2048,128]{1,0:T(8,128)(2,1)} %get-tuple-element.9.part), custom_call_target="tpu_custom_call" | custom-call | tf_op jit(solution)/shard_map/weight_reduce/pallas_call | solution.py:493
  139.9 2.2 %copy.18 = f32[648,384]{1,0:T(8,128)} copy(f32[648,384]{1,0:T(8,128)} %weight_reduce.1) | data formatting | bytes 1990656
  (1 shorter events, 0.0 us)
Async XLA Ops:
  0.6 3.8 %copy-start = (f32[32,32,9]{1,0,2:T(8,128)S(1)}, f32[32,32,9]{1,0,2:T(8,128)}, u32[]{:S(2)}) copy-start(f32[32,32,9]{1,0,2:T(8,128)} %param.9) | copy-start | bytes 110596
  5.6 1.2 copy-start.1
